TPU v7x, 512 devices: a whole 4x4x16 slice. The times are simulated.
512 devices in a mesh: group: 16 (over z), sub: 32 (over y, x, core).
Axes of the slice: x: 4, y: 4, z: 16, core: 2. Of those that a mesh axis runs over, the one named last changes fastest.
Arguments:
- points: float32 [3, 1048576], P(None, ('group', 'sub')), may hold values from 0 to 1
- leaf_basis: bfloat16 [1048576, 64], P(('group', 'sub')), as said below
- inner_transfer: bfloat16 [983040, 64], P(('group', 'sub'))
- device_transfer: float32 [32768, 64], P(('group', 'sub'))
- vectors: bfloat16 [1048576, 384], P(('group', 'sub')), may hold values from -0.75 to 0.75
- near_index: int32 [16384, 12], P(('group', 'sub')), may hold values from 0 to 16383, as said below
- near_count: int32 [16384], P(('group', 'sub')), may hold values from 6 to 12, as said below
- far_index: int32 [16384, 3], P(('group', 'sub')), may hold values from 0 to 16383, as said below
Outputs:
- near_product: bfloat16 [1048576, 384], P(('group', 'sub'))
- coupling: bfloat16 [3145728, 64], P(('group', 'sub'))
- device_factor: float32 [32768, 64], P(('group', 'sub'))
- group_factor: float32 [32768, 64], P(('group', 'sub'))
- root_factor: float32 [32768, 64], P(('group', 'sub'))
Inputs may be any that keep to these rules, and one draw needn't show every extreme that they name: Slot 0 of near_index[t] is t; the first near_count[t] slots name distinct leaves of layers t // 4 - 1 to t // 4 + 1, all within 7 of t; the remaining slots hold t. far_index[t] names 3 distinct leaves of the window of 15 consecutive leaves centred on t (moved to lie inside 0 to 16383) whose layers differ from t's by two or more. near_count[t] is at most the number of leaves in layers t // 4 - 1 to t // 4 + 1. `leaf_basis`: each leaf's block has full column rank.
All inputs are finite; a program needn't handle non-finite values.
Results may differ from a plain program's by a relative error of at most 0.005.
Values may be sent and summed in bfloat16 or wider, within the bound.
A program may use at most 64 MiB of HBM per device.

v0:
```python
import jax
import jax.numpy as jnp
from jax import lax
from jax.sharding import PartitionSpec as P

LAYER = 4
RAD = 7


SHORT_SQ = 0.09
LONG_SQ = 2.25
LONG_WEIGHT = 0.5


def from_behind(block, axis, distance):
    devices = range(lax.axis_size(axis))
    route = [(i - distance, i) for i in devices if i - distance in devices]
    return lax.ppermute(block, axis, route)


def partner_2(value, axis, bit):
    mask = 2**bit
    pairs = [(source, source ^ mask) for source in range(lax.axis_size(axis))]
    return lax.ppermute(value, axis, pairs)


def gram_matrix(matrix):
    return jnp.einsum("...ik,...il->...kl", matrix, matrix, precision=lax.Precision.HIGHEST)


def upper_factor(gram):
    return jnp.swapaxes(jnp.linalg.cholesky(gram), -1, -2)


def product(left_side, right_side):
    return jnp.einsum("...ij,...jk->...ik", left_side, right_side, precision=lax.Precision.HIGHEST)


def local_tree(leaf_factor, inner_blocks):
    factor = leaf_factor
    node_count = leaf_factor.shape[-3]
    levels = node_count.bit_length() - 1
    offset = 0
    for level in range(levels):
        merged = (gram_matrix(factor[..., 0::2, :, :]) + gram_matrix(factor[..., 1::2, :, :])) * 0.5
        factor = upper_factor(merged)
        node_count = node_count // 2
        if level + 1 < levels:
            factor = product(factor, inner_blocks[..., offset : offset + node_count, :, :])
            offset = offset + node_count
    return factor[..., 0, :, :]


def cell_offset(target, source):
    across = target % 2 - source % 2
    along = target // 2 % 2 - source // 2 % 2
    layer_gap = target // LAYER - source // LAYER
    return jnp.stack([across, along, layer_gap], axis=-1).astype(jnp.float32)


def leaf_kernel(first_pts, second_pts, offsets):
    differences = (
        first_pts[..., :, :, None] - second_pts[..., :, None, :] + offsets[..., :, None, None]
    )
    distance = jnp.sum(differences * differences, axis=-3)
    return jnp.exp(distance * (-0.5 / SHORT_SQ)) + LONG_WEIGHT * jnp.exp(
        distance * (-0.5 / LONG_SQ)
    )


def per_device(
    points, leaf_basis, inner_transfer, device_transfer, vectors, near_index, near_count, far_index
):
    leaves = near_index.shape[0]
    rank_width = leaf_basis.shape[1]
    leaf_points = leaf_basis.shape[0] // leaves
    near_slots = near_index.shape[1]
    far_slots = far_index.shape[1]
    columns = vectors.shape[1]
    first_leaf = lax.axis_index(("group", "sub")) * leaves
    blocks = vectors.reshape(leaves, leaf_points, columns)
    left_vectors = from_behind(blocks[leaves - LAYER :], ("group", "sub"), 1)
    right_vectors = from_behind(blocks[:LAYER], ("group", "sub"), -1)
    coords = points.reshape(3, leaves, leaf_points).transpose(1, 0, 2)
    basis_local = leaf_basis.astype(jnp.float32).reshape(leaves, leaf_points, rank_width)
    leaf_factor = upper_factor(gram_matrix(basis_local))
    left_factor, left_coords = (
        from_behind(leaf_factor[leaves - RAD :].astype(jnp.bfloat16), ("group", "sub"), 1).astype(
            jnp.float32
        ),
        from_behind(coords[leaves - RAD :].astype(jnp.bfloat16), ("group", "sub"), 1).astype(
            jnp.float32
        ),
    )
    right_factor, right_coords = (
        from_behind(leaf_factor[:RAD].astype(jnp.bfloat16), ("group", "sub"), -1).astype(
            jnp.float32
        ),
        from_behind(coords[:RAD].astype(jnp.bfloat16), ("group", "sub"), -1).astype(jnp.float32),
    )
    inner_blocks = inner_transfer.astype(jnp.float32).reshape(leaves - 2, rank_width, rank_width)
    subtree_top = local_tree(leaf_factor, inner_blocks)
    device_factor = product(subtree_top, device_transfer)
    factor = device_factor
    for tree_level in range(lax.axis_size("sub").bit_length() - 1):
        partner = partner_2(factor, "sub", tree_level)
        factor = upper_factor((gram_matrix(factor) + gram_matrix(partner)) * 0.5)
    group_factor = factor
    for tree_level in range(lax.axis_size("group").bit_length() - 1):
        partner = partner_2(factor, "group", tree_level)
        factor = upper_factor((gram_matrix(factor) + gram_matrix(partner)) * 0.5)
    wide_vectors = jnp.concatenate([left_vectors, blocks, right_vectors], axis=0)
    wide_coords = jnp.concatenate([left_coords, coords, right_coords], axis=0)
    wide_factor = jnp.concatenate([left_factor, leaf_factor, right_factor], axis=0)
    vector_base = first_leaf - LAYER
    coord_base = first_leaf - RAD
    near_vector_local = near_index - vector_base
    near_coord_local = near_index - coord_base
    far_local = far_index - coord_base
    target = first_leaf + jnp.arange(leaves, dtype=jnp.int32)

    def add_slot(slot_index, running):
        source = jnp.take(near_index, slot_index, axis=1)
        coord_local = jnp.take(near_coord_local, slot_index, axis=1)
        vector_local = jnp.take(near_vector_local, slot_index, axis=1)
        weights = leaf_kernel(
            coords, jnp.take(wide_coords, coord_local, axis=0), cell_offset(target, source)
        )
        weights = jnp.where((slot_index < near_count)[:, None, None], weights, 0.0).astype(
            jnp.bfloat16
        )
        gathered = jnp.take(wide_vectors, vector_local, axis=0)
        return running + jnp.einsum(
            "lij,ljv->liv", weights, gathered, preferred_element_type=jnp.float32
        )

    near_total = lax.fori_loop(
        0, near_slots, add_slot, jnp.zeros((leaves, leaf_points, columns), jnp.float32)
    )
    near_product = near_total.astype(jnp.bfloat16).reshape(leaves * leaf_points, columns)
    pieces = []
    for slot_index in range(far_slots):
        source_local = far_local[:, slot_index]
        source = far_index[:, slot_index]
        kernel_block = leaf_kernel(
            coords, jnp.take(wide_coords, source_local, axis=0), cell_offset(target, source)
        )
        other_factor = jnp.take(wide_factor, source_local, axis=0)
        projected = (
            product(product(leaf_factor, kernel_block), jnp.swapaxes(other_factor, -1, -2))
            / rank_width
        )
        pieces.append(projected)
    coupling = (
        jnp.stack(pieces, axis=1)
        .astype(jnp.bfloat16)
        .reshape(leaves * far_slots * rank_width, rank_width)
    )
    return (near_product, coupling, device_factor, group_factor, factor)


def solution(mesh):
    placed = (
        P(None, ("group", "sub")),
        P(("group", "sub"), None),
        P(("group", "sub"), None),
        P(("group", "sub"), None),
        P(("group", "sub"), None),
        P(("group", "sub"), None),
        P(("group", "sub")),
        P(("group", "sub"), None),
    )
    return jax.shard_map(
        per_device,
        mesh=mesh,
        in_specs=placed,
        out_specs=(
            P(("group", "sub"), None),
            P(("group", "sub"), None),
            P(("group", "sub"), None),
            P(("group", "sub"), None),
            P(("group", "sub"), None),
        ),
        check_vma=False,
    )
```

profile of v0, /device:TPU:8, one launch (start us, length us, event | category | flops | bytes accessed | tf_op | source)
XLA Modules:
  0.0 705.8 jit_solution(4146329838330627310)
XLA Ops:
  9.9 5.7 collective-permute-start.3
  21.6 187.5 %custom-call.26 = f32[32,64,64]{2,1,0:T(8,128)S(1)} custom-call(f32[32,64,64]{2,1,0:T(8,128)S(1)} %fusion.47), custom_call_target="Cholesky" | custom-call | tf_op jit(solution)/shard_map/jit(cholesky)/cholesky | solution.py:32
  216.1 94.5 %custom-call.27 = f32[16,64,64]{2,1,0:T(8,128)S(1)} custom-call(f32[16,64,64]{2,1,0:T(8,128)} %fusion.73), custom_call_target="Cholesky" | custom-call | tf_op jit(solution)/shard_map/jit(cholesky)/cholesky | solution.py:32
  312.9 46.9 %custom-call.28 = f32[8,64,64]{2,1,0:T(8,128)S(1)} custom-call(f32[8,64,64]{2,1,0:T(8,128)S(1)} %fusion.109), custom_call_target="Cholesky" | custom-call | tf_op jit(solution)/shard_map/jit(cholesky)/cholesky | solution.py:32
  361.3 23.5 %custom-call.29 = f32[4,64,64]{2,1,0:T(8,128)S(1)} custom-call(f32[4,64,64]{2,1,0:T(8,128)S(1)} %fusion.120), custom_call_target="Cholesky" | custom-call | tf_op jit(solution)/shard_map/jit(cholesky)/cholesky | solution.py:32
  386.0 11.9 %custom-call.30 = f32[2,64,64]{2,1,0:T(8,128)S(1)} custom-call(f32[2,64,64]{2,1,0:T(8,128)S(1)} %fusion.131), custom_call_target="Cholesky" | custom-call | tf_op jit(solution)/shard_map/jit(cholesky)/cholesky | solution.py:32
  399.0 5.9 custom-call.31
  410.1 5.7 collective-permute-start.5
  433.8 5.8 cholesky.372
  447.1 5.8 cholesky.383
  461.9 5.8 cholesky.394
  490.5 5.8 cholesky.405
  497.7 5.4 collective-permute-start.10
  505.3 5.8 cholesky.416
  512.4 10.8 %collective-permute-start.11 = (f32[64,64]{0,1:T(8,128)S(1)}, f32[64,64]{0,1:T(8,128)S(1)}, u32[]{:S(2)}, u32[]{:S(2)}) collective-permute-start(f32[64,64]{0,1:T(8,128)S(1)} %fusion.170), channel_id=1, source_target_pairs={{0,32},{32,0},{64,96},{96,64},{128,160},{160,128},{192,224},{224,1... | collective-permute-start | bytes 49160 | tf_op jit(solution)/shard_map/ppermute | solution.py:24
  525.2 5.8 cholesky.427
  532.4 5.4 collective-permute-start.12
  539.9 5.8 cholesky.438
  547.1 11.1 %collective-permute-start.13 = (f32[64,64]{0,1:T(8,128)S(1)}, f32[64,64]{0,1:T(8,128)S(1)}, u32[]{:S(2)}, u32[]{:S(2)}) collective-permute-start(f32[64,64]{0,1:T(8,128)S(1)} %fusion.173), channel_id=1, source_target_pairs={{0,128},{32,160},{64,192},{96,224},{128,0},{160,32},{192,64},{224,... | collective-permute-start | bytes 49160 | tf_op jit(solution)/shard_map/ppermute | solution.py:24
  560.4 5.8 cholesky.449
  567.5 15.0 %collective-permute-start.14 = (f32[64,64]{0,1:T(8,128)S(1)}, f32[64,64]{0,1:T(8,128)S(1)}, u32[]{:S(2)}, u32[]{:S(2)}) collective-permute-start(f32[64,64]{0,1:T(8,128)S(1)} %fusion.175), channel_id=1, source_target_pairs={{0,256},{32,288},{64,320},{96,352},{128,384},{160,416},{192,448},{... | collective-permute-start | bytes 49160 | tf_op jit(solution)/shard_map/ppermute | solution.py:24
  584.7 5.8 cholesky.460
  595.2 106.9 %while.22 = (s32[]{:T(128)}, f32[32,64,384]{2,1,0:T(8,128)}, s32[32]{0:T(128)S(1)}, f32[32,3,64]{2,1,0:T(4,128)S(1)}, s32[32,12]{0,1:T(8,128)S(1)}, /*index=5*/f...) while((s32[]{:T(128)}, f32[32,64,384]{2,1,0:T(8,128)}, ...), condition=%wide.region_2.5_spmd.clone.clone.clone, body=%wide.region_0.4_spmd.clone.clone.clone.sunk | while | flops 105262984 | bytes 12218532 | solution.py:137
  634.2 4.4 select_add_fusion.2
  (366 shorter events, 216.5 us)
Async XLA Ops:
  0.6 404.9 %copy-start = (f32[64,64]{1,0:T(8,128)S(1)}, f32[64,64]{1,0:T(8,128)}, u32[]{:S(2)}) copy-start(f32[64,64]{1,0:T(8,128)} %param.20) | copy-start | bytes 49156
  2.1 408.0 %collective-permute-start.1 = (bf16[7,3,64]{2,1,0:T(4,128)(2,1)}, bf16[7,3,64]{2,1,0:T(4,128)(2,1)}, u32[]{:S(2)}, u32[]{:S(2)}) collective-permute-start(bf16[7,3,64]{2,1,0:T(4,128)(2,1)} %get-tuple-element.576), channel_id=1, source_target_pairs={{1,0},{2,1},{3,2},{4,3},{5,4},{6,5},{7,6},{8,7},{9,8},{10,9},{11,1... | collective-permute-start | bytes 8072 | tf_op jit(solution)/shard_map/ppermute | solution.py:18
  6.1 410.5 %collective-permute-start = (bf16[7,3,64]{2,1,0:T(4,128)(2,1)S(1)}, bf16[7,3,64]{2,1,0:T(4,128)(2,1)}, u32[]{:S(2)}, u32[]{:S(2)}) collective-permute-start(bf16[7,3,64]{2,1,0:T(4,128)(2,1)S(1)} %get-tuple-element.575), channel_id=1, source_target_pairs={{0,1},{1,2},{2,3},{3,4},{4,5},{5,6},{6,7},{7,8},{8,9},{9,10},{10,1... | collective-permute-start | bytes 8072 | tf_op jit(solution)/shard_map/ppermute | solution.py:18
  9.9 582.7 %collective-permute-start.3 = (bf16[4,64,384]{2,1,0:T(8,128)(2,1)}, bf16[4,64,384]{2,1,0:T(8,128)(2,1)}, u32[]{:S(2)}, u32[]{:S(2)}) collective-permute-start(bf16[4,64,384]{2,1,0:T(8,128)(2,1)} %bitcast.3), channel_id=1, source_target_pairs={{1,0},{2,1},{3,2},{4,3},{5,4},{6,5},{7,6},{8,7},{9,8},{10,9},{11,1... | collective-permute-start | bytes 589832 | tf_op jit(solution)/shard_map/ppermute | solution.py:18
  15.6 576.9 %collective-permute-start.2 = (bf16[4,64,384]{2,1,0:T(8,128)(2,1)}, bf16[4,64,384]{2,1,0:T(8,128)(2,1)}, u32[]{:S(2)}, u32[]{:S(2)}) collective-permute-start(bf16[4,64,384]{2,1,0:T(8,128)(2,1)} %bitcast.1), channel_id=1, source_target_pairs={{0,1},{1,2},{2,3},{3,4},{4,5},{5,6},{6,7},{7,8},{8,9},{9,10},{10,1... | collective-permute-start | bytes 589832 | tf_op jit(solution)/shard_map/ppermute | solution.py:18
  21.4 188.1 %slice-start = ((bf16[1920,64]{0,1:T(8,128)(2,1)}), bf16[128,64]{0,1:T(8,128)(2,1)S(1)}, s32[]{:S(2)}) async-start(bf16[1920,64]{0,1:T(8,128)(2,1)} %param.19), calls=%async_computation | async-start | bytes 32768 | tf_op jit(solution)/shard_map/slice | solution.py:49
  21.4 188.2 %slice-start.1 = ((bf16[1920,64]{0,1:T(8,128)(2,1)}), bf16[256,64]{0,1:T(8,128)(2,1)S(1)}, s32[]{:S(2)}) async-start(bf16[1920,64]{0,1:T(8,128)(2,1)} %param.19), calls=%async_computation.1 | async-start | bytes 65536 | tf_op jit(solution)/shard_map/slice | solution.py:49
  21.4 188.9 %slice-start.2 = ((bf16[1920,64]{0,1:T(8,128)(2,1)}), bf16[512,64]{0,1:T(8,128)(2,1)S(1)}, s32[]{:S(2)}) async-start(bf16[1920,64]{0,1:T(8,128)(2,1)} %param.19), calls=%async_computation.2 | async-start | bytes 131072 | tf_op jit(solution)/shard_map/slice | solution.py:49
  310.8 49.1 %copy-start.5 = (bf16[512,64]{1,0:T(8,128)(2,1)S(1)}, bf16[512,64]{1,0:T(8,128)(2,1)}, u32[]{:S(2)}) copy-start(bf16[512,64]{1,0:T(8,128)(2,1)} %copy.265) | copy-start | bytes 196612
  312.7 72.3 %copy-start.7 = (bf16[256,64]{1,0:T(8,128)(2,1)S(1)}, bf16[256,64]{1,0:T(8,128)(2,1)}, u32[]{:S(2)}) copy-start(bf16[256,64]{1,0:T(8,128)(2,1)} %copy.272) | copy-start | bytes 98308
  359.9 48.7 %copy-start.9 = (s32[32,3]{0,1:T(4,128)S(1)}, s32[32,3]{0,1:T(4,128)}, u32[]{:S(2)}) copy-start(s32[32,3]{0,1:T(4,128)} %param.24) | copy-start | bytes 1156
  360.4 49.4 %copy-start.8 = (s32[32,12]{0,1:T(8,128)S(1)}, s32[32,12]{0,1:T(8,128)}, u32[]{:S(2)}) copy-start(s32[32,12]{0,1:T(8,128)} %param.22) | copy-start | bytes 4612
  406.5 27.0 %collective-permute-start.6 = (f32[64,64]{1,0:T(8,128)S(1)}, f32[64,64]{1,0:T(8,128)S(1)}, u32[]{:S(2)}, u32[]{:S(2)}) collective-permute-start(f32[64,64]{1,0:T(8,128)S(1)} %fusion.143), channel_id=1, source_target_pairs={{0,1},{1,0},{2,3},{3,2},{4,5},{5,4},{6,7},{7,6},{8,9},{9,8},{10,11... | collective-permute-start | bytes 49160 | tf_op jit(solution)/shard_map/ppermute | solution.py:24
  410.1 61.7 %collective-permute-start.5 = (bf16[7,64,64]{1,2,0:T(8,128)(2,1)S(1)}, bf16[7,64,64]{1,2,0:T(8,128)(2,1)S(1)}, u32[]{:S(2)}, u32[]{:S(2)}) collective-permute-start(bf16[7,64,64]{1,2,0:T(8,128)(2,1)S(1)} %get-tuple-element.574), channel_id=1, source_target_pairs={{1,0},{2,1},{3,2},{4,3},{5,4},{6,5},{7,6},{8,7},{9,8},{10,9},{11,1... | collective-permute-start | bytes 172040 | tf_op jit(solution)/shard_map/ppermute | solution.py:18
  416.6 55.3 %collective-permute-start.4 = (bf16[7,64,64]{1,2,0:T(8,128)(2,1)S(1)}, bf16[7,64,64]{1,2,0:T(8,128)(2,1)S(1)}, u32[]{:S(2)}, u32[]{:S(2)}) collective-permute-start(bf16[7,64,64]{1,2,0:T(8,128)(2,1)S(1)} %get-tuple-element.573), channel_id=1, source_target_pairs={{0,1},{1,2},{2,3},{3,4},{4,5},{5,6},{6,7},{7,8},{8,9},{9,10},{10,1... | collective-permute-start | bytes 172040 | tf_op jit(solution)/shard_map/ppermute | solution.py:18
  441.0 5.8 collective-permute-start.7
  454.3 7.3 %collective-permute-start.8 = (f32[64,64]{0,1:T(8,128)S(1)}, f32[64,64]{0,1:T(8,128)S(1)}, u32[]{:S(2)}, u32[]{:S(2)}) collective-permute-start(f32[64,64]{0,1:T(8,128)S(1)} %fusion.163), channel_id=1, source_target_pairs={{0,4},{1,5},{2,6},{3,7},{4,0},{5,1},{6,2},{7,3},{8,12},{9,13},{10,... | collective-permute-start | bytes 49160 | tf_op jit(solution)/shard_map/ppermute | solution.py:24
  469.9 20.2 %collective-permute-start.9 = (f32[64,64]{0,1:T(8,128)S(1)}, f32[64,64]{0,1:T(8,128)S(1)}, u32[]{:S(2)}, u32[]{:S(2)}) collective-permute-start(f32[64,64]{0,1:T(8,128)S(1)} %fusion.165), channel_id=1, source_target_pairs={{0,8},{1,9},{2,10},{3,11},{4,12},{5,13},{6,14},{7,15},{8,0},{9,1},... | collective-permute-start | bytes 49160 | tf_op jit(solution)/shard_map/ppermute | solution.py:24
  490.2 102.4 %copy-start.4 = (bf16[2048,384]{1,0:T(8,128)(2,1)S(1)}, bf16[2048,384]{1,0:T(8,128)(2,1)}, u32[]{:S(2)}) copy-start(bf16[2048,384]{1,0:T(8,128)(2,1)} %param.21) | copy-start | bytes 4718596
  497.7 7.3 %collective-permute-start.10 = (f32[64,64]{0,1:T(8,128)S(1)}, f32[64,64]{0,1:T(8,128)S(1)}, u32[]{:S(2)}, u32[]{:S(2)}) collective-permute-start(f32[64,64]{0,1:T(8,128)S(1)} %fusion.167), channel_id=1, source_target_pairs={{0,16},{1,17},{2,18},{3,19},{4,20},{5,21},{6,22},{7,23},{8,24},{9,... | collective-permute-start | bytes 49160 | tf_op jit(solution)/shard_map/ppermute | solution.py:24
  512.4 12.5 %collective-permute-start.11 = (f32[64,64]{0,1:T(8,128)S(1)}, f32[64,64]{0,1:T(8,128)S(1)}, u32[]{:S(2)}, u32[]{:S(2)}) collective-permute-start(f32[64,64]{0,1:T(8,128)S(1)} %fusion.170), channel_id=1, source_target_pairs={{0,32},{32,0},{64,96},{96,64},{128,160},{160,128},{192,224},{224,1... | collective-permute-start | bytes 49160 | tf_op jit(solution)/shard_map/ppermute | solution.py:24
  532.4 7.2 %collective-permute-start.12 = (f32[64,64]{0,1:T(8,128)S(1)}, f32[64,64]{0,1:T(8,128)S(1)}, u32[]{:S(2)}, u32[]{:S(2)}) collective-permute-start(f32[64,64]{0,1:T(8,128)S(1)} %fusion.171), channel_id=1, source_target_pairs={{0,64},{32,96},{64,0},{96,32},{128,192},{160,224},{192,128},{224,1... | collective-permute-start | bytes 49160 | tf_op jit(solution)/shard_map/ppermute | solution.py:24
  547.1 13.0 %collective-permute-start.13 = (f32[64,64]{0,1:T(8,128)S(1)}, f32[64,64]{0,1:T(8,128)S(1)}, u32[]{:S(2)}, u32[]{:S(2)}) collective-permute-start(f32[64,64]{0,1:T(8,128)S(1)} %fusion.173), channel_id=1, source_target_pairs={{0,128},{32,160},{64,192},{96,224},{128,0},{160,32},{192,64},{224,... | collective-permute-start | bytes 49160 | tf_op jit(solution)/shard_map/ppermute | solution.py:24
  567.5 16.8 %collective-permute-start.14 = (f32[64,64]{0,1:T(8,128)S(1)}, f32[64,64]{0,1:T(8,128)S(1)}, u32[]{:S(2)}, u32[]{:S(2)}) collective-permute-start(f32[64,64]{0,1:T(8,128)S(1)} %fusion.175), channel_id=1, source_target_pairs={{0,256},{32,288},{64,320},{96,352},{128,384},{160,416},{192,448},{... | collective-permute-start | bytes 49160 | tf_op jit(solution)/shard_map/ppermute | solution.py:24
  (5 other events, 27.4 us)
where the time goes:
time: 717 us; the launch traced here: 706 us
  other arithmetic  468 us (65%)
  matrix products  82.9 us (12%)
  starting transfers between devices  77.1 us (11%)
  local copies, waits for them, and re-layouts  63.7 us (9%)
  waiting for transfers between devices  11.3 us (2%)
    another operation x46, other arithmetic, upper_factor(): return jnp.swapaxes(jnp.linalg.cholesky(gram), -1, -2)  430 us
    ppermute x9, starting transfers between devices, partner_2(): return lax.ppermute(value, axis, pairs)  55.9 us
    dot_general x12, matrix products, add_slot(): jnp.einsum('lij,ljv->liv', weights, gathered, preferred_element_type=jnp....  51.4 us
    gather x12, local copies, waits for them, and re-layouts, add_slot(): gathered = jnp.take(wide_vectors, vector_local, axis=0)  29.2 us
    ppermute x6, starting transfers between devices, from_behind(): return lax.ppermute(block, axis, route)  21.2 us
    reduce_sum x13, other arithmetic, leaf_kernel(): distance = jnp.sum(differences * differences, axis=-3)  17.7 us
    dot_general x11, matrix products, product(): jnp.einsum('...ij,...jk->...ik', left_side, right_side, precision=lax.Pre...  17.6 us
  transfers between devices with their start and end apart: 15, of which 7 were waited for; matrix products, arithmetic and copies ran while one was open for 71% of the time, Pallas kernels for 0%

commit v1 on v0

v1 whole, which is shorter than its diff:
```python
import functools
import math

import jax
import jax.numpy as jnp
from jax import lax
from jax.experimental import pallas as pl
from jax.experimental.pallas import tpu as pltpu
from jax.sharding import PartitionSpec as P

K = 64
LAYER = 4
HALO = 8
OWN = 32
WIDE = OWN + 2 * HALO
SHORT_SQ = 0.09
LONG_SQ = 2.25
RATIO = LONG_SQ / SHORT_SQ
SCALE = math.sqrt(0.5 / LONG_SQ * math.log2(math.e))
OFF = -1.0e5
VMEM_LIMIT = 48 << 20
F32 = jnp.float32
BF16 = jnp.bfloat16


def shifted(block, axis, distance):
    devices = range(lax.axis_size(axis))
    route = [(i - distance, i) for i in devices if i - distance in devices]
    return lax.ppermute(block, axis, route)


def dot(a, b):
    return jnp.dot(a, b, preferred_element_type=F32)


def dot_t(a, b):
    return lax.dot_general(a, b, (((0,), (0,)), ((), ())), preferred_element_type=F32)


def dot_nt(a, b):
    return lax.dot_general(a, b, (((1,), (1,)), ((), ())), preferred_element_type=F32)


def exact_dot(a, b):
    return jnp.dot(a, b, preferred_element_type=F32, precision=lax.Precision.HIGHEST)


def exact_dot_t(a, b):
    return lax.dot_general(
        a, b, (((0,), (0,)), ((), ())), preferred_element_type=F32, precision=lax.Precision.HIGHEST
    )


def split3(x):
    high = x.astype(BF16)
    rest = x - high.astype(F32)
    middle = rest.astype(BF16)
    low = (rest - middle.astype(F32)).astype(BF16)
    return high, middle, low


def split2(x):
    high = x.astype(BF16)
    return high, (x - high.astype(F32)).astype(BF16)


def wide_dot(exact, x):
    high, middle, low = split3(x)
    return dot(exact, high) + (dot(exact, middle) + dot(exact, low))


def cholesky_rows(a_ref):
    lanes = a_ref.shape[2]
    for block in range(K // 4):
        first = 4 * block
        start = first // 8 * 8
        rows = tuple(a_ref[first + q, start:K, :] for q in range(4))

        def subtract(k, rows):
            done = a_ref[k, start:K, :]
            return tuple(
                rows[q] - a_ref[k, first + q : first + q + 1, :] * done for q in range(4)
            )

        if first:
            rows = lax.fori_loop(0, first, subtract, rows, unroll=4)
        rows = list(rows)
        index = lax.broadcasted_iota(jnp.int32, (K - start, lanes), 0)
        for q in range(4):
            at = first + q - start
            row = rows[q] * lax.rsqrt(rows[q][at : at + 1, :])
            row = jnp.where(index >= at, row, 0.0)
            a_ref[first + q, start:K, :] = row
            if start:
                a_ref[first + q, 0:start, :] = jnp.zeros((start, lanes), F32)
            for other in range(q + 1, 4):
                into = first + other - start
                rows[other] = rows[other] - row[into : into + 1, :] * row


def tree_kernel(basis_ref, inner_ref, transfer_ref, leaf_ref, factor_ref, gram_ref, g_ref, a_ref):
    slots = a_ref.shape[2]
    path = [inner_ref[(28 + m) * K : (29 + m) * K, :].astype(F32) for m in range(2)]
    for first, count in ((24, 4), (16, 8), (0, 16)):
        longer = []
        for m in range(count // 2):
            rows = inner_ref[(first + 2 * m) * K : (first + 2 * m + 2) * K, :]
            both = wide_dot(rows, path[m])
            longer += [both[:K], both[K:]]
        path = longer
    top = jnp.zeros((K, K), F32)
    for m in range(16):
        x = wide_dot(basis_ref[2 * m * K : (2 * m + 2) * K, :], path[m])
        top = top + exact_dot_t(x, x)
    top = top * (1.0 / OWN)
    transfer = transfer_ref[...]
    gram_ref[...] = exact_dot_t(transfer, exact_dot(top, transfer))
    for t in range(OWN):
        v = basis_ref[t * K : (t + 1) * K, :]
        g_ref[t * K : (t + 1) * K, :] = dot_t(v, v)
    for t in range(OWN, slots):
        g_ref[t * K : (t + 1) * K, :] = top
    for i in range(K):
        a_ref[i] = g_ref[pl.ds(i, slots, stride=K), :].T
    cholesky_rows(a_ref)
    for i in range(K):
        g_ref[pl.ds(i, slots, stride=K), :] = a_ref[i].T
    leaf_ref[...] = g_ref[0 : OWN * K, :]
    factor_ref[...] = exact_dot(g_ref[OWN * K : (OWN + 1) * K, :], transfer)


def tree_call(leaf_basis, inner_transfer, device_transfer):
    slots = 40
    whole = pl.BlockSpec(memory_space=pltpu.VMEM)
    return pl.pallas_call(
        tree_kernel,
        out_shape=(
            jax.ShapeDtypeStruct((OWN * K, K), F32),
            jax.ShapeDtypeStruct((K, K), F32),
            jax.ShapeDtypeStruct((K, K), F32),
        ),
        in_specs=[whole] * 3,
        out_specs=(whole,) * 3,
        scratch_shapes=[
            pltpu.VMEM((slots * K, K), F32),
            pltpu.VMEM((K, K, slots), F32),
        ],
        compiler_params=pltpu.CompilerParams(vmem_limit_bytes=VMEM_LIMIT),
    )(leaf_basis, inner_transfer, device_transfer)


def final_kernel(group_ref, root_ref, group_out, root_out, a_ref):
    for i in range(K):
        lane = lax.broadcasted_iota(jnp.int32, (K, 128), 1)
        a_ref[i] = jnp.where(lane < 64, group_ref[:, i : i + 1], root_ref[:, i : i + 1])
    cholesky_rows(a_ref)
    lane = lax.broadcasted_iota(jnp.int32, (K, 128), 1)
    group_t = jnp.zeros((K, 128), F32)
    root_t = jnp.zeros((K, 128), F32)
    for i in range(K):
        row = a_ref[i]
        group_t = jnp.where(lane == i, row, group_t)
        root_t = jnp.where(lane == i + 64, row, root_t)
    group_out[...] = group_t.T[:K, :]
    root_out[...] = root_t.T[K:, :]


def final_call(group_gram, root_gram):
    whole = pl.BlockSpec(memory_space=pltpu.VMEM)
    return pl.pallas_call(
        final_kernel,
        out_shape=(jax.ShapeDtypeStruct((K, K), F32),) * 2,
        in_specs=[whole] * 2,
        out_specs=(whole,) * 2,
        scratch_shapes=[pltpu.VMEM((K, K, 128), F32)],
        compiler_params=pltpu.CompilerParams(vmem_limit_bytes=VMEM_LIMIT),
    )(group_gram, root_gram)


def kernel_values(exponent):
    return jnp.exp2(exponent * RATIO) + 0.5 * jnp.exp2(exponent)


def field_kernel(
    coords_ref,
    near_ref,
    count_ref,
    far_ref,
    left_ref,
    own_ref,
    right_ref,
    factor_ref,
    near_out,
    coupling_out,
    source_ref,
    target_ref,
    leaf_source_ref,
    index_ref,
    off_ref,
    factor_high,
    factor_low,
    block_ref,
    half_ref,
):
    first_leaf = (lax.axis_index("group") * lax.axis_size("sub") + lax.axis_index("sub")) * OWN
    lanes = WIDE * K
    leaf = lax.broadcasted_iota(jnp.int32, (1, lanes), 1) // K
    corners = (leaf % 2, leaf // 2 % 2, leaf // LAYER - WIDE // LAYER // 2)
    ones = jnp.ones((1, lanes), F32)
    target_rows, source_rows, norm = [], [], jnp.zeros((1, lanes), F32)
    for c in range(3):
        u = (coords_ref[c : c + 1, :] + corners[c].astype(F32)) * SCALE
        high, middle, low = (part.astype(F32) for part in split3(u))
        norm = norm - u * u
        for a, b in (
            (high, high),
            (high, middle),
            (middle, high),
            (high, low),
            (low, high),
            (middle, middle),
        ):
            target_rows.append(2.0 * a)
            source_rows.append(b)
    for part in split3(norm):
        target_rows += [part.astype(F32), ones]
        source_rows += [ones, part.astype(F32)]
    for p in range(LAYER):
        target_rows.append((leaf % LAYER == p).astype(F32))
        source_rows.append(jnp.zeros((1, lanes), F32))
    for _ in range(4):
        target_rows.append(jnp.zeros((1, lanes), F32))
        source_rows.append(jnp.zeros((1, lanes), F32))
    for r in range(32):
        source_ref[r : r + 1, :] = source_rows[r]
    for r in range(32):
        target_rows[r] = target_rows[r][:, HALO * K : (HALO + OWN) * K]
    targets = jnp.concatenate(target_rows, axis=0)
    target_ref[...] = targets.T.astype(BF16)
    for w in range(WIDE):
        leaf_source_ref[w] = source_ref[:, w * K : (w + 1) * K].astype(BF16)

    slot = lax.broadcasted_iota(jnp.int32, (8, 128), 1)
    row = lax.broadcasted_iota(jnp.int32, (8, 128), 0)
    for layer in range(OWN // LAYER):
        index_ref[...] = jnp.full((8, 128), -1, jnp.int32)
        index_ref[0:LAYER, 0:12] = near_ref[LAYER * layer : LAYER * (layer + 1), :]
        used = jnp.zeros((8, 128), jnp.int32)
        for p in range(LAYER):
            used = jnp.where(row == p, count_ref[LAYER * layer + p], used)
        place = index_ref[...] - (first_leaf + LAYER * (layer - 1))
        place = jnp.where(slot < used, place, -1)
        present = jnp.zeros((8, 128), jnp.bool_)
        for n in range(12):
            present = present | (place[:, n : n + 1] == slot)
        bias = jnp.where(present | (row >= LAYER), 0.0, OFF)
        for pair in range(6):
            off_ref[layer, :, pair * 128 : (pair + 1) * 128] = jnp.where(
                slot < K, bias[:, 2 * pair : 2 * pair + 1], bias[:, 2 * pair + 1 : 2 * pair + 2]
            )

    def vectors(layer):
        if layer < 0:
            return left_ref[...]
        if layer >= OWN // LAYER:
            return right_ref[...]
        return own_ref[layer * LAYER * K : (layer + 1) * LAYER * K, :]

    width = LAYER * K
    for layer in range(OWN // LAYER):
        total = jnp.zeros((width, own_ref.shape[1]), F32)
        for step in range(3):
            at = (layer + 1 + step) * width
            source = jnp.concatenate(
                [
                    source_ref[0:24, at : at + width],
                    source_ref[24:32, at : at + width]
                    + off_ref[layer, :, step * width : (step + 1) * width],
                ],
                axis=0,
            ).astype(BF16)
            exponent = dot(target_ref[layer * width : (layer + 1) * width, :], source)
            weights = kernel_values(exponent).astype(BF16)
            total = total + dot(weights, vectors(layer - 1 + step))
        near_out[layer * width : (layer + 1) * width, :] = total.astype(BF16)

    for w in range(WIDE):
        high, low = split2(factor_ref[w * K : (w + 1) * K, :])
        factor_high[w] = high
        factor_low[w] = low

    def blocks(pair, _):
        t = pair // 3
        w = far_ref[t, pair - 3 * t] - first_leaf + HALO
        exponent = dot(target_ref[pl.ds(t * K, K), :], leaf_source_ref[w])
        high, low = split2(kernel_values(exponent))
        block_ref[pair, 0] = high
        block_ref[pair, 1] = low
        return 0

    lax.fori_loop(0, 3 * OWN, blocks, 0, unroll=4)

    def halves(pair, _):
        t = pair // 3
        high, low = factor_high[t + HALO], factor_low[t + HALO]
        s_high, s_low = block_ref[pair, 0], block_ref[pair, 1]
        half = dot(high, s_high) + (dot(high, s_low) + dot(low, s_high))
        half_high, half_low = split2(half * (1.0 / K))
        half_ref[pair, 0] = half_high
        half_ref[pair, 1] = half_low
        return 0

    lax.fori_loop(0, 3 * OWN, halves, 0, unroll=4)

    def projected(pair, _):
        t = pair // 3
        w = far_ref[t, pair - 3 * t] - first_leaf + HALO
        high, low = factor_high[w], factor_low[w]
        h_high, h_low = half_ref[pair, 0], half_ref[pair, 1]
        value = dot_nt(h_high, high) + (dot_nt(h_high, low) + dot_nt(h_low, high))
        coupling_out[pl.ds(pair * K, K), :] = value.astype(BF16)
        return 0

    lax.fori_loop(0, 3 * OWN, projected, 0, unroll=4)


def field_call(coords, near_index, near_count, far_index, left, own, right, factors):
    whole = pl.BlockSpec(memory_space=pltpu.VMEM)
    scalars = pl.BlockSpec(memory_space=pltpu.SMEM)
    return pl.pallas_call(
        field_kernel,
        out_shape=(
            jax.ShapeDtypeStruct(own.shape, BF16),
            jax.ShapeDtypeStruct((3 * OWN * K, K), BF16),
        ),
        in_specs=[whole, whole, scalars, scalars, whole, whole, whole, whole],
        out_specs=(whole, whole),
        scratch_shapes=[
            pltpu.VMEM((32, WIDE * K), F32),
            pltpu.VMEM((OWN * K, 32), BF16),
            pltpu.VMEM((WIDE, 32, K), BF16),
            pltpu.VMEM((8, 128), jnp.int32),
            pltpu.VMEM((OWN // LAYER, 8, 12 * K), F32),
            pltpu.VMEM((WIDE, K, K), BF16),
            pltpu.VMEM((WIDE, K, K), BF16),
            pltpu.VMEM((3 * OWN, 2, K, K), BF16),
            pltpu.VMEM((3 * OWN, 2, K, K), BF16),
        ],
        compiler_params=pltpu.CompilerParams(vmem_limit_bytes=VMEM_LIMIT),
    )(coords, near_index, near_count, far_index, left, own, right, factors)


def per_device(
    points, leaf_basis, inner_transfer, device_transfer, vectors, near_index, near_count, far_index
):
    both = ("group", "sub")
    edge = HALO * K
    left_vectors = shifted(vectors[-LAYER * K :], both, 1)
    right_vectors = shifted(vectors[: LAYER * K], both, -1)
    left_points = shifted(points[:, -edge:], both, 1)
    right_points = shifted(points[:, :edge], both, -1)
    leaf_factor, device_factor, device_gram = tree_call(leaf_basis, inner_transfer, device_transfer)
    left_factor = shifted(leaf_factor[-edge:], both, 1)
    right_factor = shifted(leaf_factor[:edge], both, -1)
    group_gram = lax.psum(device_gram, "sub") * (1.0 / lax.axis_size("sub"))
    root_gram = lax.psum(group_gram, "group") * (1.0 / lax.axis_size("group"))
    coords = jnp.concatenate([left_points, points, right_points], axis=1)
    factors = jnp.concatenate([left_factor, leaf_factor, right_factor], axis=0)
    near_product, coupling = field_call(
        coords, near_index, near_count, far_index, left_vectors, vectors, right_vectors, factors
    )
    group_factor, root_factor = final_call(group_gram, root_gram)
    return near_product, coupling, device_factor, group_factor, root_factor


def solution(mesh):
    rows = P(("group", "sub"), None)
    return jax.shard_map(
        per_device,
        mesh=mesh,
        in_specs=(
            P(None, ("group", "sub")),
            rows,
            rows,
            rows,
            rows,
            rows,
            P(("group", "sub")),
            rows,
        ),
        out_specs=(rows,) * 5,
        check_vma=False,
    )
```

time: 717 us -> 265 us (0.37)
  the two profiles are of different devices: /device:TPU:8 before, /device:TPU:1 now
where the time goes in v1:
time: 265 us; the launch traced here: 264 us
  blocking collectives  179 us (68%)
  starting transfers between devices  38.6 us (15%)
  Pallas kernels  36.5 us (14%)
  local copies, waits for them, and re-layouts  8.2 us (3%)
    psum x1, blocking collectives, per_device(): group_gram = lax.psum(device_gram, 'sub') * (1.0 / lax.axis_size('sub'))  130 us
    psum x1, blocking collectives, per_device(): root_gram = lax.psum(group_gram, 'group') * (1.0 / lax.axis_size('group'))  49 us
    ppermute x6, starting transfers between devices, shifted(): return lax.ppermute(block, axis, route)  38.6 us
    pallas_call x1, Pallas kernels, field_call(): pl.pallas_call(field_kernel, out_shape=(jax.ShapeDtypeStruct(own.shape, B...  22.5 us
    pallas_call x1, Pallas kernels, tree_call(): pl.pallas_call(tree_kernel, out_shape=(jax.ShapeDtypeStruct((OWN * K, K),...  8.99 us
    unnamed x19, local copies, waits for them, and re-layouts  6.65 us
  transfers between devices with their start and end apart: 6, of which 0 were waited for; matrix products, arithmetic and copies ran while one was open for 1% of the time, Pallas kernels for 2%

profile of v1, /device:TPU:1, one launch (start us, length us, event | category | flops | bytes accessed | tf_op | source)
XLA Modules:
  0.0 264.2 jit_solution(3428178235707991087)
XLA Ops:
  0.6 1.2 copy.13.basis_ref
  1.9 0.0 copy-start
  1.9 2.1 copy.14.inner_ref
  3.9 1.0 copy-done.1
  5.0 0.8 copy-done.2
  5.7 9.0 %shard_map.119 = (f32[2048,64]{1,0:T(8,128)S(1)}, f32[64,64]{1,0:T(8,128)}, f32[64,64]{1,0:T(8,128)S(1)}) custom-call(bf16[2048,64]{1,0:T(8,128)(2,1)S(1)} %copy.13.basis_ref, bf16[1920,64]{1,0:T(8,128)(2,1)S(1)} %copy-done.1, f32[64,64]{1,0:T(8,128)S(1)} %copy-done.2), custom_call_target="tpu_custom_call" | custom-call | tf_op jit(solution)/shard_map/pallas_call | solution.py:135
  14.7 0.8 fusion.1
  15.5 4.5 %collective-permute-start.4 = (f32[512,64]{1,0:T(8,128)}, f32[512,64]{1,0:T(8,128)S(1)}, u32[]{:S(2)}, u32[]{:S(2)}) collective-permute-start(f32[512,64]{1,0:T(8,128)} %get-tuple-element.26), channel_id=1, source_target_pairs={{0,1},{1,2},{2,3},{3,4},{4,5},{5,6},{6,7},{7,8},{8,9},{9,10},{10,1... | collective-permute-start | bytes 393224 | tf_op jit(solution)/shard_map/ppermute | solution.py:29
  20.0 5.6 %collective-permute-start.5 = (f32[512,64]{1,0:T(8,128)}, f32[512,64]{1,0:T(8,128)}, u32[]{:S(2)}, u32[]{:S(2)}) collective-permute-start(f32[512,64]{1,0:T(8,128)} %get-tuple-element.27), channel_id=1, source_target_pairs={{1,0},{2,1},{3,2},{4,3},{5,4},{6,5},{7,6},{8,7},{9,8},{10,9},{11,1... | collective-permute-start | bytes 393224 | tf_op jit(solution)/shard_map/ppermute | solution.py:29
  25.7 1.9 collective-permute-start
  27.6 2.4 collective-permute-start.1
  30.0 0.7 fusion
  30.7 3.1 %collective-permute-start.2 = (bf16[256,384]{1,0:T(8,128)(2,1)}, bf16[256,384]{1,0:T(8,128)(2,1)S(1)}, u32[]{:S(2)}, u32[]{:S(2)}) collective-permute-start(bf16[256,384]{1,0:T(8,128)(2,1)} %get-tuple-element.25), channel_id=1, source_target_pairs={{0,1},{1,2},{2,3},{3,4},{4,5},{5,6},{6,7},{7,8},{8,9},{9,10},{10,1... | collective-permute-start | bytes 589832 | tf_op jit(solution)/shard_map/ppermute | solution.py:29
  33.9 129.9 %psum.14 = f32[64,64]{1,0:T(8,128)S(1)} all-reduce(f32[64,64]{1,0:T(8,128)S(1)} %get-tuple-element.16), channel_id=1, replica_groups=mesh['group'=16,'sub'=32] {'sub'}, use_global_device_ids=true, to_apply=%region_0.0 | all-reduce | flops 4096 | bytes 32768 | tf_op jit(solution)/shard_map/psum | solution.py:365
  163.8 49.0 %psum.15 = f32[64,64]{1,0:T(8,128)S(1)} all-reduce(f32[64,64]{1,0:T(8,128)S(1)} %broadcast_multiply_fusion.1.group_ref), channel_id=1, replica_groups=mesh['group'=16,'sub'=32] {'group'}, use_global_device_ids=true, to_apply=%region_1.0 | all-reduce | flops 4096 | bytes 32768 | tf_op jit(solution)/shard_map/psum | solution.py:366
  212.8 0.1 copy.15.near_ref
  212.9 0.1 copy.16.far_ref
  213.0 5.1 %shard_map.121 = (f32[64,64]{1,0:T(8,128)}, f32[64,64]{1,0:T(8,128)}) custom-call(f32[64,64]{1,0:T(8,128)S(1)} %broadcast_multiply_fusion.1.group_ref, f32[64,64]{1,0:T(8,128)S(1)} %broadcast_multiply_fusion.root_ref), custom_call_target="tpu_custom_call" | custom-call | tf_op jit(solution)/shard_map/pallas_call | solution.py:170
  218.1 21.1 %collective-permute-start.3 = (bf16[256,384]{1,0:T(8,128)(2,1)S(1)}, bf16[256,384]{1,0:T(8,128)(2,1)S(1)}, u32[]{:S(2)}, u32[]{:S(2)}) collective-permute-start(bf16[256,384]{1,0:T(8,128)(2,1)S(1)} %get-tuple-element.24), channel_id=1, source_target_pairs={{1,0},{2,1},{3,2},{4,3},{5,4},{6,5},{7,6},{8,7},{9,8},{10,9},{11,1... | collective-permute-start | bytes 589832 | tf_op jit(solution)/shard_map/ppermute | solution.py:29
  239.2 0.0 copy-start.3
  239.2 0.0 collective-permute-done.4
  239.2 1.1 pad_maximum_fusion.factor_ref
  240.3 22.5 %shard_map.120 = (bf16[2048,384]{1,0:T(8,128)(2,1)}, bf16[6144,64]{1,0:T(8,128)(2,1)S(1)}) custom-call(f32[3,3072]{1,0:T(4,128)S(1)} %pad_maximum_fusion.1.coords_ref, s32[32,12]{1,0:T(8,128)S(1)} %copy.15.near_ref, s32[32]{0:T(128)S(1)} %copy-done.3, s32[32,3]{1,0:T(8,128)S(1)} %copy.16.far_ref, bf16[256,384]{1,0:T(8,128)(2,1)S(1)} %collective-permute-done.2.left_ref, ...), custom_call_target="tpu_custom_call" | custom-call | tf_op jit(solution)/shard_map/pallas_call | solution.py:330
  262.8 1.4 copy.17
  (19 shorter events, 0.1 us)
Async XLA Ops:
  1.9 28.1 %copy-start = (bf16[2048,384]{1,0:T(8,128)(2,1)S(1)}, bf16[2048,384]{1,0:T(8,128)(2,1)}, u32[]{:S(2)}) copy-start(bf16[2048,384]{1,0:T(8,128)(2,1)} %own_ref.1) | copy-start | bytes 4718596
  3.9 1.0 copy-start.1
  5.0 0.8 copy-start.2
  5.7 19.9 %copy-start.4 = (f32[3,2048]{1,0:T(4,128)S(1)}, f32[3,2048]{1,0:T(4,128)}, u32[]{:S(2)}) copy-start(f32[3,2048]{1,0:T(4,128)} %param.8) | copy-start | bytes 73732
  5.7 207.1 %copy-start.5 = (s32[32,12]{0,1:T(8,128)S(1)}, s32[32,12]{0,1:T(8,128)}, u32[]{:S(2)}) copy-start(s32[32,12]{0,1:T(8,128)} %param.13) | copy-start | bytes 4612
  5.7 207.2 %copy-start.6 = (s32[32,3]{0,1:T(4,128)S(1)}, s32[32,3]{0,1:T(4,128)}, u32[]{:S(2)}) copy-start(s32[32,3]{0,1:T(4,128)} %param.15) | copy-start | bytes 1156
  15.5 223.7 %collective-permute-start.4 = (f32[512,64]{1,0:T(8,128)}, f32[512,64]{1,0:T(8,128)S(1)}, u32[]{:S(2)}, u32[]{:S(2)}) collective-permute-start(f32[512,64]{1,0:T(8,128)} %get-tuple-element.26), channel_id=1, source_target_pairs={{0,1},{1,2},{2,3},{3,4},{4,5},{5,6},{6,7},{7,8},{8,9},{9,10},{10,1... | collective-permute-start | bytes 393224 | tf_op jit(solution)/shard_map/ppermute | solution.py:29
  20.0 219.2 %collective-permute-start.5 = (f32[512,64]{1,0:T(8,128)}, f32[512,64]{1,0:T(8,128)}, u32[]{:S(2)}, u32[]{:S(2)}) collective-permute-start(f32[512,64]{1,0:T(8,128)} %get-tuple-element.27), channel_id=1, source_target_pairs={{1,0},{2,1},{3,2},{4,3},{5,4},{6,5},{7,6},{8,7},{9,8},{10,9},{11,1... | collective-permute-start | bytes 393224 | tf_op jit(solution)/shard_map/ppermute | solution.py:29
  25.7 192.4 %collective-permute-start = (f32[3,512]{1,0:T(4,128)S(1)}, f32[3,512]{1,0:T(4,128)S(1)}, u32[]{:S(2)}, u32[]{:S(2)}) collective-permute-start(f32[3,512]{1,0:T(4,128)S(1)} %get-tuple-element.28), channel_id=1, source_target_pairs={{0,1},{1,2},{2,3},{3,4},{4,5},{5,6},{6,7},{7,8},{8,9},{9,10},{10,1... | collective-permute-start | bytes 18440 | tf_op jit(solution)/shard_map/ppermute | solution.py:29
  27.6 211.6 %collective-permute-start.1 = (f32[3,512]{1,0:T(4,128)S(1)}, f32[3,512]{1,0:T(4,128)S(1)}, u32[]{:S(2)}, u32[]{:S(2)}) collective-permute-start(f32[3,512]{1,0:T(4,128)S(1)} %get-tuple-element.29), channel_id=1, source_target_pairs={{1,0},{2,1},{3,2},{4,3},{5,4},{6,5},{7,6},{8,7},{9,8},{10,9},{11,1... | collective-permute-start | bytes 18440 | tf_op jit(solution)/shard_map/ppermute | solution.py:29
  30.7 209.6 %collective-permute-start.2 = (bf16[256,384]{1,0:T(8,128)(2,1)}, bf16[256,384]{1,0:T(8,128)(2,1)S(1)}, u32[]{:S(2)}, u32[]{:S(2)}) collective-permute-start(bf16[256,384]{1,0:T(8,128)(2,1)} %get-tuple-element.25), channel_id=1, source_target_pairs={{0,1},{1,2},{2,3},{3,4},{4,5},{5,6},{6,7},{7,8},{8,9},{9,10},{10,1... | collective-permute-start | bytes 589832 | tf_op jit(solution)/shard_map/ppermute | solution.py:29
  218.1 22.2 %collective-permute-start.3 = (bf16[256,384]{1,0:T(8,128)(2,1)S(1)}, bf16[256,384]{1,0:T(8,128)(2,1)S(1)}, u32[]{:S(2)}, u32[]{:S(2)}) collective-permute-start(bf16[256,384]{1,0:T(8,128)(2,1)S(1)} %get-tuple-element.24), channel_id=1, source_target_pairs={{1,0},{2,1},{3,2},{4,3},{5,4},{6,5},{7,6},{8,7},{9,8},{10,9},{11,1... | collective-permute-start | bytes 589832 | tf_op jit(solution)/shard_map/ppermute | solution.py:29
  239.2 1.1 copy-start.3

commit v2 on v1

v2 whole, which is shorter than its diff:
```python
import math

import jax
import jax.numpy as jnp
from jax import lax
from jax.experimental import pallas as pl
from jax.experimental.pallas import tpu as pltpu
from jax.sharding import PartitionSpec as P

K = 64
PAIR = 2 * K
LAYER = 4
NEAR = 12
FAR = 3
HALO = 8
OWN = 32
WIDE = OWN + 2 * HALO
EDGE = HALO * K
SLOTS = 40
SHORT_SQ = 0.09
LONG_SQ = 2.25
RATIO = LONG_SQ / SHORT_SQ
SCALE = math.sqrt(0.5 / LONG_SQ * math.log2(math.e))
OFF = -131072.0
VMEM_LIMIT = 48 << 20
F32 = jnp.float32
BF16 = jnp.bfloat16
MESH = pl.DeviceIdType.MESH
ROUNDS = 5
SENT = 13


def dot(a, b):
    return jnp.dot(a, b, preferred_element_type=F32)


def dot_nt(a, b):
    return lax.dot_general(a, b, (((1,), (1,)), ((), ())), preferred_element_type=F32)


def exact_dot(a, b):
    return jnp.dot(a, b, preferred_element_type=F32, precision=lax.Precision.HIGHEST)


def exact_dot_t(a, b):
    return lax.dot_general(
        a, b, (((0,), (0,)), ((), ())), preferred_element_type=F32, precision=lax.Precision.HIGHEST
    )


def split3(x):
    high = x.astype(BF16)
    rest = x - high.astype(F32)
    middle = rest.astype(BF16)
    low = (rest - middle.astype(F32)).astype(BF16)
    return high, middle, low


def dot_wide(x, exact):
    rows = x.shape[0]
    parts = dot(jnp.concatenate(split3(x), axis=0), exact)
    return parts[:rows] + (parts[rows : 2 * rows] + parts[2 * rows :])


def in_first_half(shape):
    return lax.broadcasted_iota(jnp.int32, shape, len(shape) - 1) < K


def high_low(doubled):
    high = doubled.astype(BF16).astype(F32)
    return jnp.where(in_first_half(doubled.shape), high, doubled - high).astype(BF16)


def add_halves(x):
    return x + pltpu.roll(x, K, axis=1)


def cholesky_rows(a_ref, blocks):
    lanes = a_ref.shape[2]
    for block in blocks:
        first = 4 * block
        start = first // 8 * 8
        rows = tuple(a_ref[first + q, start:K, :] for q in range(4))

        def subtract(k, rows):
            done = a_ref[k, start:K, :]
            return tuple(
                rows[q] - a_ref[k, first + q : first + q + 1, :] * done for q in range(4)
            )

        if first:
            rows = lax.fori_loop(0, first, subtract, rows, unroll=4)
        rows = list(rows)
        index = lax.broadcasted_iota(jnp.int32, (K - start, lanes), 0)
        for q in range(4):
            at = first + q - start
            row = rows[q] * lax.rsqrt(rows[q][at : at + 1, :])
            row = jnp.where(index >= at, row, 0.0)
            a_ref[first + q, start:K, :] = row
            if start:
                a_ref[first + q, 0:start, :] = jnp.zeros((start, lanes), F32)
            for other in range(q + 1, 4):
                into = first + other - start
                rows[other] = rows[other] - row[into : into + 1, :] * row


def tree_gram(basis_ref, inner_ref, x_ref):
    last = inner_ref[:, 14 * PAIR : 15 * PAIR].astype(F32)
    path = [last[:, :K], last[:, K:]]
    for first, count in ((12, 4), (8, 8), (0, 16)):
        longer = []
        for m in range(count // 2):
            both = dot_wide(path[m], inner_ref[:, (first + m) * PAIR : (first + m + 1) * PAIR])
            longer += [both[:, :K], both[:, K:]]
        path = longer
    for m in range(16):
        x = dot_wide(path[m], basis_ref[:, m * PAIR : (m + 1) * PAIR])
        for part, value in enumerate(split3(x)):
            x_ref[part * K : (part + 1) * K, m * PAIR : (m + 1) * PAIR] = value
    parts = dot_nt(x_ref[0:PAIR, :], x_ref[...])
    parts = parts[:K] + parts[K:]
    low = parts[:, PAIR : PAIR + K]
    return (parts[:, :K] + parts[:, K:PAIR] + (low + low.T)) * (1.0 / OWN)


def unpack(ref):
    return jnp.concatenate([ref[:, :K], ref[:, K:]], axis=0)


def upsweep_kernel(
    basis_ref,
    inner_ref,
    transfer_ref,
    points_ref,
    vectors_ref,
    factor_out,
    group_out,
    root_out,
    pairs_out,
    own_pairs_out,
    left_points,
    right_points,
    left_vectors,
    right_vectors,
    g_ref,
    d_ref,
    a_ref,
    last_ref,
    x_ref,
    sum_ref,
    got_ref,
    send_sem,
    recv_sem,
):
    groups, subs = lax.axis_size("group"), lax.axis_size("sub")
    g, s = lax.axis_index("group"), lax.axis_index("sub")
    me = g * subs + s
    after = lax.rem(me + 1, groups * subs)
    before = lax.rem(me + groups * subs - 1, groups * subs)
    after = (after // subs, lax.rem(after, subs))
    before = (before // subs, lax.rem(before, subs))

    def turned(index, stride, size, by):
        at = lax.rem(index // stride, size)
        return index + (lax.rem(at + by, size) - at) * stride

    rounds = [
        [(g, turned(s, 1, 2, 1))],
        [(g, turned(s, 2, 4, by)) for by in (1, 2, 3)],
        [(g, turned(s, 8, 4, by)) for by in (1, 2, 3)],
        [(turned(g, 1, 4, by), s) for by in (1, 2, 3)],
        [(turned(g, 4, 4, by), s) for by in (1, 2, 3)],
    ]
    offsets = [0, 1, 4, 7, 10]

    barrier = pltpu.get_barrier_semaphore()
    greeted = [after, before] + [device for stage in rounds for device in stage]
    for device in greeted:
        pl.semaphore_signal(barrier, inc=1, device_id=device, device_id_type=MESH)
    pl.semaphore_wait(barrier, len(greeted))

    def copy(number, source, target, device):
        return pltpu.make_async_remote_copy(
            src_ref=source,
            dst_ref=target,
            send_sem=send_sem.at[number],
            recv_sem=recv_sem.at[number],
            device_id=device,
            device_id_type=MESH,
        )

    rows, lanes = vectors_ref.shape[0], points_ref.shape[1]
    halos = [
        copy(SENT, vectors_ref.at[rows - LAYER * K : rows], left_vectors, after),
        copy(SENT + 1, vectors_ref.at[0 : LAYER * K], right_vectors, before),
        copy(SENT + 2, points_ref.at[:, lanes - EDGE : lanes], left_points, after),
        copy(SENT + 3, points_ref.at[:, 0:EDGE], right_points, before),
    ]
    for halo in halos:
        halo.start()

    def send(stage):
        copies = [
            copy(offsets[stage] + n, sum_ref.at[stage], got_ref.at[offsets[stage] + n], device)
            for n, device in enumerate(rounds[stage])
        ]
        for one in copies:
            one.start()
        return copies

    def receive(stage, copies):
        total = sum_ref[stage]
        for n, one in enumerate(copies):
            one.wait()
            total = total + got_ref[offsets[stage] + n]
        sum_ref[stage + 1] = total

    top = tree_gram(basis_ref, inner_ref, x_ref)
    transfer = transfer_ref[...]
    gram = exact_dot_t(transfer, exact_dot(top, transfer))
    sum_ref[0] = jnp.concatenate([gram[: K // 2], gram[K // 2 :]], axis=1)
    sent = send(0)

    first = in_first_half((K, PAIR))
    for m in range(OWN // 2):
        v = basis_ref[:, m * PAIR : (m + 1) * PAIR]
        zero = jnp.zeros_like(v)
        one_each = jnp.concatenate([jnp.where(first, v, zero), jnp.where(first, zero, v)], axis=0)
        g_ref[m * PAIR : (m + 1) * PAIR, :] = dot_nt(one_each, v)
    for t in range(OWN, SLOTS):
        g_ref[t * K : (t + 1) * K, :] = top
    receive(0, sent)
    sent = send(1)
    for i in range(K):
        a_ref[i] = g_ref[pl.ds(i, SLOTS, stride=K), :].T
    receive(1, sent)
    sent = send(2)
    cholesky_rows(a_ref, range(0, 7))
    receive(2, sent)
    sent = send(3)
    cholesky_rows(a_ref, range(7, 16))
    receive(3, sent)
    sent = send(4)
    for i in range(K):
        row = a_ref[i]
        d_ref[pl.ds(i, SLOTS, stride=K), :] = jnp.concatenate([row, row], axis=0).T
    for t in range(OWN):
        doubled = d_ref[t * K : (t + 1) * K, :]
        high = doubled.astype(BF16).astype(F32)
        low = doubled - high
        pair = jnp.where(first, high, low).astype(BF16)
        pairs_out[EDGE + t * K : EDGE + (t + 1) * K, :] = pair
        own_pairs_out[t * PAIR : t * PAIR + K, :] = pair
        own_pairs_out[t * PAIR + K : (t + 1) * PAIR, :] = jnp.where(first, low, high).astype(BF16)
    edges = [
        copy(SENT + 4, pairs_out.at[OWN * K : OWN * K + EDGE], pairs_out.at[0:EDGE], after),
        copy(
            SENT + 5,
            pairs_out.at[EDGE : 2 * EDGE],
            pairs_out.at[OWN * K + EDGE : OWN * K + 2 * EDGE],
            before,
        ),
    ]
    for edge in edges:
        edge.start()
    factor_out[...] = exact_dot(d_ref[OWN * K : (OWN + 1) * K, 0:K], transfer)
    receive(4, sent)

    group = unpack(sum_ref[3]) * (1.0 / subs)
    root = unpack(sum_ref[5]) * (1.0 / (subs * groups))
    for i in range(K):
        last_ref[i] = jnp.where(first, group[:, i : i + 1], root[:, i : i + 1])
    cholesky_rows(last_ref, range(16))
    lane = lax.broadcasted_iota(jnp.int32, (K, PAIR), 1)
    columns = jnp.zeros((K, PAIR), F32)
    others = jnp.zeros((K, PAIR), F32)
    for i in range(K):
        row = last_ref[i]
        columns = jnp.where(lane == i, row, columns)
        others = jnp.where(lane == i + K, row, others)
    group_out[...] = columns.T[:K, :]
    root_out[...] = others.T[K:, :]
    for done in halos + edges:
        done.wait()


def upsweep_call(basis_t, inner_t, transfer, points, vectors):
    whole = pl.BlockSpec(memory_space=pltpu.VMEM)
    anywhere = pl.BlockSpec(memory_space=pl.ANY)
    square = jax.ShapeDtypeStruct((K, K), F32)
    edge_points = jax.ShapeDtypeStruct((points.shape[0], EDGE), F32)
    edge_vectors = jax.ShapeDtypeStruct((LAYER * K, vectors.shape[1]), BF16)
    copies = SENT + 6
    return pl.pallas_call(
        upsweep_kernel,
        out_shape=(
            square,
            square,
            square,
            jax.ShapeDtypeStruct((WIDE * K, PAIR), BF16),
            jax.ShapeDtypeStruct((OWN * PAIR, PAIR), BF16),
            edge_points,
            edge_points,
            edge_vectors,
            edge_vectors,
        ),
        in_specs=[whole] * 4 + [anywhere],
        out_specs=(whole,) * 7 + (anywhere,) * 2,
        scratch_shapes=[
            pltpu.VMEM((SLOTS * K, K), F32),
            pltpu.VMEM((SLOTS * K, PAIR), F32),
            pltpu.VMEM((K, K, SLOTS), F32),
            pltpu.VMEM((K, K, PAIR), F32),
            pltpu.VMEM((3 * K, OWN * K), BF16),
            pltpu.VMEM((ROUNDS + 1, K // 2, PAIR), F32),
            pltpu.VMEM((SENT, K // 2, PAIR), F32),
            pltpu.SemaphoreType.DMA((copies,)),
            pltpu.SemaphoreType.DMA((copies,)),
        ],
        compiler_params=pltpu.CompilerParams(
            collective_id=0, has_side_effects=True, vmem_limit_bytes=VMEM_LIMIT
        ),
    )(basis_t, inner_t, transfer, points, vectors)


def kernel_values(exponent):
    return jnp.exp2(exponent * RATIO) + 0.5 * jnp.exp2(exponent)


def field_kernel(
    left_points,
    points_ref,
    right_points,
    near_ref,
    count_ref,
    far_ref,
    left_ref,
    own_ref,
    right_ref,
    pairs_ref,
    own_pairs_ref,
    factor_ref,
    group_ref,
    root_ref,
    near_out,
    coupling_out,
    factor_out,
    group_out,
    root_out,
    coords_ref,
    source_ref,
    target_ref,
    source_t_ref,
    target_t_ref,
    doubled_ref,
    block_ref,
    half_ref,
):
    factor_out[...] = factor_ref[...]
    group_out[...] = group_ref[...]
    root_out[...] = root_ref[...]
    first_leaf = (lax.axis_index("group") * lax.axis_size("sub") + lax.axis_index("sub")) * OWN
    lanes = WIDE * K
    coords_ref[:, 0:EDGE] = left_points[...]
    coords_ref[:, EDGE : lanes - EDGE] = points_ref[...]
    coords_ref[:, lanes - EDGE : lanes] = right_points[...]
    leaf = lax.broadcasted_iota(jnp.int32, (3, lanes), 1) // K
    axis = lax.broadcasted_iota(jnp.int32, (3, lanes), 0)
    corner = jnp.where(
        axis == 0, leaf % 2, jnp.where(axis == 1, leaf // 2 % 2, leaf // LAYER - WIDE // LAYER // 2)
    )
    u = (coords_ref[...] + corner.astype(F32)) * SCALE
    high, middle, low = (part.astype(F32) for part in split3(u))
    norms = [part.astype(F32) for part in split3(-jnp.sum(u * u, axis=0, keepdims=True))]
    ones = jnp.ones((3, lanes), F32)
    own = slice(EDGE, lanes - EDGE)
    for n, (a, b) in enumerate(
        (
            (high, high),
            (high, middle),
            (middle, high),
            (high, low),
            (low, high),
            (middle, middle),
        )
    ):
        target_ref[3 * n : 3 * n + 3, :] = 2.0 * a[:, own]
        source_ref[3 * n : 3 * n + 3, :] = b
    target_ref[18:21, :] = ones[:, own]
    source_ref[21:24, :] = ones
    for n, part in enumerate(norms):
        source_ref[18 + n : 19 + n, :] = part
        target_ref[21 + n : 22 + n, :] = part[:, own]
    source_ref[24:32, :] = jnp.zeros((8, lanes), F32)

    slot = lax.broadcasted_iota(jnp.int32, (NEAR, OWN), 0)
    target = lax.broadcasted_iota(jnp.int32, (NEAR, OWN), 1)
    used = jnp.zeros((NEAR, OWN), jnp.int32)
    for t in range(OWN):
        used = jnp.where(target == t, count_ref[t], used)
    place = near_ref[...] - (first_leaf - LAYER) - target // LAYER * LAYER
    place = jnp.where(slot < used, place, -1)
    window = lax.broadcasted_iota(jnp.int32, (16, OWN), 0)
    bias = jnp.full((16, OWN), OFF, F32)
    for n in range(NEAR):
        bias = jnp.where(place[n : n + 1, :] == window, 0.0, bias)
    spread = lax.broadcasted_iota(jnp.int32, (OWN, OWN * K), 1) // K
    spread = (spread == lax.broadcasted_iota(jnp.int32, (OWN, OWN * K), 0)).astype(F32)
    target_ref[24:40, :] = dot(bias.astype(BF16), spread.astype(BF16))

    target_t_ref[...] = target_ref[...].T.astype(BF16)
    source_t_ref[...] = source_ref[...].T.astype(BF16)
    for t in range(OWN):
        one = target_ref[0:32, t * K : (t + 1) * K]
        doubled_ref[t] = jnp.concatenate([one, one], axis=1).astype(BF16)

    def vectors(layer):
        if layer < 0:
            return left_ref[...]
        if layer >= OWN // LAYER:
            return right_ref[...]
        return own_ref[layer * LAYER * K : (layer + 1) * LAYER * K, :]

    width = LAYER * K
    window = lax.broadcasted_iota(jnp.int32, (16, width), 0)
    column = lax.broadcasted_iota(jnp.int32, (16, width), 1) // K
    for layer in range(OWN // LAYER):
        total = jnp.zeros((width, own_ref.shape[1]), F32)
        for step in range(3):
            at = (layer + 1 + step) * width
            place = (window == column + LAYER * step).astype(F32)
            source = jnp.concatenate([source_ref[0:24, at : at + width], place], axis=0)
            exponent = dot(
                target_t_ref[layer * width : (layer + 1) * width, :], source.astype(BF16)
            )
            weights = kernel_values(exponent).astype(BF16)
            total = total + dot(weights, vectors(layer - 1 + step))
        near_out[layer * width : (layer + 1) * width, :] = total.astype(BF16)

    def leaf_rows(ref, leaf, rows):
        return ref[pl.ds(pl.multiple_of(leaf * rows, rows), rows), :]

    def blocks(t, _):
        sources = [
            leaf_rows(source_t_ref, far_ref[f, t] - first_leaf + HALO, K) for f in range(FAR)
        ]
        exponent = dot(jnp.concatenate(sources, axis=0), doubled_ref[t])
        block_ref[t] = high_low(kernel_values(exponent))
        return 0

    lax.fori_loop(0, OWN, blocks, 0, unroll=4)

    def halves(t, _):
        value = dot_nt(block_ref[t], leaf_rows(own_pairs_ref, t, PAIR))
        half_ref[t] = high_low(add_halves(value) * (1.0 / K))
        return 0

    lax.fori_loop(0, OWN, halves, 0, unroll=4)

    def projected(pair, _):
        values = []
        for t in (2 * pair, 2 * pair + 1):
            for f in range(FAR):
                half = half_ref[t, f * K : (f + 1) * K, :]
                pairs = leaf_rows(pairs_ref, far_ref[f, t] - first_leaf + HALO, K)
                values.append(add_halves(dot(pairs, jnp.concatenate([half, half], axis=0))))
        first = in_first_half((K, PAIR))
        both = [jnp.where(first, values[2 * n], values[2 * n + 1]) for n in range(FAR)]
        at = pl.multiple_of(pair * FAR * PAIR, PAIR)
        coupling_out[:, pl.ds(at, FAR * PAIR)] = jnp.concatenate(both, axis=1).astype(BF16)
        return 0

    lax.fori_loop(0, OWN // 2, projected, 0, unroll=2)


def field_call(left, points, right, near_t, near_count, far_t, *rest):
    whole = pl.BlockSpec(memory_space=pltpu.VMEM)
    scalars = pl.BlockSpec(memory_space=pltpu.SMEM)
    vectors = rest[1]
    square = jax.ShapeDtypeStruct((K, K), F32)
    return pl.pallas_call(
        field_kernel,
        out_shape=(
            jax.ShapeDtypeStruct(vectors.shape, BF16),
            jax.ShapeDtypeStruct((K, FAR * OWN * K), BF16),
            square,
            square,
            square,
        ),
        in_specs=[whole] * 4 + [scalars] * 2 + [whole] * len(rest),
        out_specs=(whole,) * 5,
        scratch_shapes=[
            pltpu.VMEM((3, WIDE * K), F32),
            pltpu.VMEM((32, WIDE * K), F32),
            pltpu.VMEM((40, OWN * K), F32),
            pltpu.VMEM((WIDE * K, 32), BF16),
            pltpu.VMEM((OWN * K, 40), BF16),
            pltpu.VMEM((OWN, 32, PAIR), BF16),
            pltpu.VMEM((OWN, FAR * K, PAIR), BF16),
            pltpu.VMEM((OWN, FAR * K, PAIR), BF16),
        ],
        compiler_params=pltpu.CompilerParams(vmem_limit_bytes=VMEM_LIMIT),
    )(left, points, right, near_t, near_count, far_t, *rest)


def per_device(
    points, leaf_basis, inner_transfer, device_transfer, vectors, near_index, near_count, far_index
):
    factor, group, root, pairs, own_pairs, left_points, right_points, left, right = upsweep_call(
        leaf_basis.T, inner_transfer.T, device_transfer, points, vectors
    )
    near_product, coupling_t, device_factor, group_factor, root_factor = field_call(
        left_points,
        points,
        right_points,
        near_index.T,
        near_count,
        far_index.T,
        left,
        vectors,
        right,
        pairs,
        own_pairs,
        factor,
        group,
        root,
    )
    return near_product, coupling_t.T, device_factor, group_factor, root_factor


def solution(mesh):
    rows = P(("group", "sub"), None)
    return jax.shard_map(
        per_device,
        mesh=mesh,
        in_specs=(
            P(None, ("group", "sub")),
            rows,
            rows,
            rows,
            rows,
            rows,
            P(("group", "sub")),
            rows,
        ),
        out_specs=(rows,) * 5,
        check_vma=False,
    )
```

time: 265 us -> 60.2 us (0.23)
  blocking collectives: 179 us -> 0 us
  starting transfers between devices: 38.6 us -> 0 us
  Pallas kernels: 36.5 us -> 53.7 us
  local copies, waits for them, and re-layouts: 8.2 us -> 4.84 us
    psum x2 -> x0, blocking collectives: 179 us -> none  [the longest x1 130 us: per_device(): group_gram = lax.psum(device_gram, 'sub') * (1.0 / lax.axis_size('sub'))]
    ppermute x6 -> x0, starting transfers between devices: 38.6 us -> none  [shifted(): return lax.ppermute(block, axis, route)]
    pallas_call x3 -> x2, Pallas kernels: 36.5 us -> 53.7 us  [the longest x1 39.6 us: upsweep_call(): pl.pallas_call(upsweep_kernel, out_shape=(square, square, square, jax.Sha...]
    unnamed x19 -> x18, local copies, waits for them, and re-layouts: 6.65 us -> 4.84 us
  transfers between devices with their start and end apart: 6 -> 0, of which waited for: 0 -> 0; matrix products, arithmetic and copies ran while one was open for 1% -> 0% of each run, Pallas kernels for 2% -> 0%
where the time goes in v2:
time: 60.2 us; the launch traced here: 59.2 us
  Pallas kernels  53.7 us (89%)
  local copies, waits for them, and re-layouts  4.84 us (8%)
  between operations  0.7 us (1%)
    pallas_call x1, Pallas kernels, upsweep_call(): pl.pallas_call(upsweep_kernel, out_shape=(square, square, square, jax.Sha...  39.6 us
    pallas_call x1, Pallas kernels, field_call(): pl.pallas_call(field_kernel, out_shape=(jax.ShapeDtypeStruct(vectors.shap...  14.1 us
    unnamed x18, local copies, waits for them, and re-layouts  4.84 us

profile of v2, /device:TPU:1, one launch (start us, length us, event | category | flops | bytes accessed | tf_op | source)
XLA Modules:
  0.0 59.2 jit_solution(1299471793592080968)
XLA Ops:
  0.6 0.0 copy-start.7
  0.6 0.0 copy-start.8
  0.7 0.0 copy-start
  0.7 1.4 %copy-done = bf16[2048,384]{1,0:T(8,128)(2,1)S(1)} copy-done((bf16[2048,384]{1,0:T(8,128)(2,1)S(1)}, bf16[2048,384]{1,0:T(8,128)(2,1)}, u32[]{:S(2)}) %copy-start) | copy-done | bytes 1572888
  2.1 0.0 copy-start.2
  2.1 0.9 %copy-done.2 = bf16[2048,64]{0,1:T(8,128)(2,1)S(1)} copy-done((bf16[2048,64]{0,1:T(8,128)(2,1)S(1)}, bf16[2048,64]{0,1:T(8,128)(2,1)}, u32[]{:S(2)}) %copy-start.2) | copy-done | bytes 262168
  3.0 0.0 copy-start.3
  3.0 0.9 %copy-done.3 = bf16[1920,64]{0,1:T(8,128)(2,1)S(1)} copy-done((bf16[1920,64]{0,1:T(8,128)(2,1)S(1)}, bf16[1920,64]{0,1:T(8,128)(2,1)}, u32[]{:S(2)}) %copy-start.3) | copy-done | bytes 245784
  4.0 0.0 copy-start.4
  4.0 0.8 %copy-done.4 = f32[3,2048]{1,0:T(4,128)S(1)} copy-done((f32[3,2048]{1,0:T(4,128)S(1)}, f32[3,2048]{1,0:T(4,128)}, u32[]{:S(2)}) %copy-start.4) | copy-done | bytes 24600
  4.7 0.0 copy-start.5
  4.7 0.8 %copy-done.5 = f32[64,64]{1,0:T(8,128)S(1)} copy-done((f32[64,64]{1,0:T(8,128)S(1)}, f32[64,64]{1,0:T(8,128)}, u32[]{:S(2)}) %copy-start.5) | copy-done | bytes 16408
  5.5 0.0 copy-start.1
  5.5 0.0 copy-start.6
  5.5 39.6 %shard_map.119 = (f32[64,64]{1,0:T(8,128)S(1)}, f32[64,64]{1,0:T(8,128)S(1)}, f32[64,64]{1,0:T(8,128)S(1)}, bf16[3072,128]{1,0:T(8,128)(2,1)S(1)}, bf16[4096,128...) custom-call(bf16[64,2048]{1,0:T(8,128)(2,1)S(1)} %bitcast.5, ...), custom_call_target="tpu_custom_call" | custom-call | tf_op jit(solution)/shard_map/pallas_call | solution.py:294
  45.1 0.0 copy-done.7
  45.1 0.0 copy-done.8
  45.1 0.0 copy-done.1
  45.1 0.0 copy-done.6
  45.1 14.1 %shard_map.120 = (bf16[2048,384]{1,0:T(8,128)(2,1)}, bf16[64,6144]{1,0:T(8,128)(2,1)}, f32[64,64]{1,0:T(8,128)}, f32[64,64]{1,0:T(8,128)}, f32[64,64]{1,0:T(8,128)}) custom-call(f32[3,512]{1,0:T(4,128)S(1)} %get-tuple-element.19.left_points, f32[3,2048]{1,0:T(4,128)S(1)} %copy-done.4, f32[3,512]{1,0:T(4,128)S(1)} %get-tuple-element.20.right_points, ...), custom_call_target="tpu_custom_call" | custom-call | tf_op jit(solution)/shard_map/pallas_call | solution.py:481
Async XLA Ops:
  0.6 44.4 %copy-start.7 = (s32[32,3]{0,1:T(4,128)S(1)}, s32[32,3]{0,1:T(4,128)}, u32[]{:S(2)}) copy-start(s32[32,3]{0,1:T(4,128)} %param.15) | copy-start | bytes 1156
  0.6 44.4 %copy-start.8 = (s32[32]{0:T(128)S(1)}, s32[32]{0:T(128)}, u32[]{:S(2)}) copy-start(s32[32]{0:T(128)} %count_ref.1) | copy-start | bytes 388
  0.7 1.4 %copy-start = (bf16[2048,384]{1,0:T(8,128)(2,1)S(1)}, bf16[2048,384]{1,0:T(8,128)(2,1)}, u32[]{:S(2)}) copy-start(bf16[2048,384]{1,0:T(8,128)(2,1)} %own_ref.1) | copy-start | bytes 4718596
  2.1 0.9 %copy-start.2 = (bf16[2048,64]{0,1:T(8,128)(2,1)S(1)}, bf16[2048,64]{0,1:T(8,128)(2,1)}, u32[]{:S(2)}) copy-start(bf16[2048,64]{0,1:T(8,128)(2,1)} %param.9) | copy-start | bytes 786436
  3.0 0.9 %copy-start.3 = (bf16[1920,64]{0,1:T(8,128)(2,1)S(1)}, bf16[1920,64]{0,1:T(8,128)(2,1)}, u32[]{:S(2)}) copy-start(bf16[1920,64]{0,1:T(8,128)(2,1)} %param.10) | copy-start | bytes 737284
  4.0 0.8 %copy-start.4 = (f32[3,2048]{1,0:T(4,128)S(1)}, f32[3,2048]{1,0:T(4,128)}, u32[]{:S(2)}) copy-start(f32[3,2048]{1,0:T(4,128)} %points_ref.3) | copy-start | bytes 73732
  4.7 0.8 %copy-start.5 = (f32[64,64]{1,0:T(8,128)S(1)}, f32[64,64]{1,0:T(8,128)}, u32[]{:S(2)}) copy-start(f32[64,64]{1,0:T(8,128)} %transfer_ref.1) | copy-start | bytes 49156
  5.5 39.6 %copy-start.1 = (bf16[2048,384]{1,0:T(8,128)(2,1)S(1)}, bf16[2048,384]{1,0:T(8,128)(2,1)}, u32[]{:S(2)}) copy-start(bf16[2048,384]{1,0:T(8,128)(2,1)} %own_ref.1) | copy-start | bytes 4718596
  5.5 39.6 %copy-start.6 = (s32[32,12]{0,1:T(8,128)S(1)}, s32[32,12]{0,1:T(8,128)}, u32[]{:S(2)}) copy-start(s32[32,12]{0,1:T(8,128)} %param.13) | copy-start | bytes 4612

commit v3 on v2

v3 whole, which is shorter than its diff:
```python
import math

import jax
import jax.numpy as jnp
from jax import lax
from jax.experimental import pallas as pl
from jax.experimental.pallas import tpu as pltpu
from jax.sharding import PartitionSpec as P

K = 64
PAIR = 2 * K
LAYER = 4
RAD = 7
NEAR = 12
FAR = 3
HALO = 8
OWN = 32
WIDE = OWN + 2 * HALO
EDGE = HALO * K
SLOTS = 40
SHORT_SQ = 0.09
LONG_SQ = 2.25
RATIO = LONG_SQ / SHORT_SQ
SCALE = math.sqrt(0.5 / LONG_SQ * math.log2(math.e))
OFF = -131072.0
VMEM_LIMIT = 60 << 20
F32 = jnp.float32
BF16 = jnp.bfloat16
MESH = pl.DeviceIdType.MESH
PLANE = 15
WINDOW = 7
COVER = 4
SUMS = PLANE + WINDOW + COVER
COPIES = SUMS + 6
INPUTS = 6
FIRST_PART = 10


def dot(a, b):
    return jnp.dot(a, b, preferred_element_type=F32)


def dot_nt(a, b):
    return lax.dot_general(a, b, (((1,), (1,)), ((), ())), preferred_element_type=F32)


def exact_dot(a, b):
    return jnp.dot(a, b, preferred_element_type=F32, precision=lax.Precision.HIGHEST)


def exact_dot_t(a, b):
    return lax.dot_general(
        a, b, (((0,), (0,)), ((), ())), preferred_element_type=F32, precision=lax.Precision.HIGHEST
    )


def split3(x):
    high = x.astype(BF16)
    rest = x - high.astype(F32)
    middle = rest.astype(BF16)
    low = (rest - middle.astype(F32)).astype(BF16)
    return high, middle, low


def dot_wide(x, exact):
    rows = x.shape[0]
    parts = dot(jnp.concatenate(split3(x), axis=0), exact)
    return parts[:rows] + (parts[rows : 2 * rows] + parts[2 * rows :])


def in_first_half(shape):
    return lax.broadcasted_iota(jnp.int32, shape, len(shape) - 1) < K


def high_low(doubled):
    high = doubled.astype(BF16).astype(F32)
    return jnp.where(in_first_half(doubled.shape), high, doubled - high).astype(BF16)


def add_halves(x):
    return x + pltpu.roll(x, K, axis=1)


def cholesky_rows(a_ref, blocks):
    lanes = a_ref.shape[2]
    for block in blocks:
        first = 4 * block
        start = first // 8 * 8
        rows = tuple(a_ref[first + q, start:K, :] for q in range(4))

        def subtract(k, rows):
            done = a_ref[k, start:K, :]
            return tuple(
                rows[q] - a_ref[k, first + q : first + q + 1, :] * done for q in range(4)
            )

        if first:
            rows = lax.fori_loop(0, first, subtract, rows, unroll=4)
        rows = list(rows)
        index = lax.broadcasted_iota(jnp.int32, (K - start, lanes), 0)
        for q in range(4):
            at = first + q - start
            row = rows[q] * lax.rsqrt(rows[q][at : at + 1, :])
            row = jnp.where(index >= at, row, 0.0)
            a_ref[first + q, start:K, :] = row
            if start:
                a_ref[first + q, 0:start, :] = jnp.zeros((start, lanes), F32)
            for other in range(q + 1, 4):
                into = first + other - start
                rows[other] = rows[other] - row[into : into + 1, :] * row


def tree_gram(basis_ref, inner_ref, x_ref):
    last = inner_ref[:, 14 * PAIR : 15 * PAIR].astype(F32)
    path = [last[:, :K], last[:, K:]]
    for first, count in ((12, 4), (8, 8), (0, 16)):
        longer = []
        for m in range(count // 2):
            both = dot_wide(path[m], inner_ref[:, (first + m) * PAIR : (first + m + 1) * PAIR])
            longer += [both[:, :K], both[:, K:]]
        path = longer
    for m in range(16):
        x = dot_wide(path[m], basis_ref[:, m * PAIR : (m + 1) * PAIR])
        for part, value in enumerate(split3(x)):
            x_ref[part * K : (part + 1) * K, m * PAIR : (m + 1) * PAIR] = value
    parts = dot_nt(x_ref[0:PAIR, :], x_ref[...])
    parts = parts[:K] + parts[K:]
    low = parts[:, PAIR : PAIR + K]
    return (parts[:, :K] + parts[:, K:PAIR] + (low + low.T)) * (1.0 / OWN)


def unpack(ref):
    return jnp.concatenate([ref[:, :K], ref[:, K:]], axis=0)


def kernel_values(exponent):
    return jnp.exp2(exponent * RATIO) + 0.5 * jnp.exp2(exponent)


def leaf_rows(ref, leaf, rows):
    return ref[pl.ds(pl.multiple_of(leaf * rows, rows), rows), :]


def leaf_grams(basis_ref, top, g_ref):
    first = in_first_half((K, PAIR))
    for m in range(OWN // 2):
        v = basis_ref[:, m * PAIR : (m + 1) * PAIR]
        zero = jnp.zeros_like(v)
        one_each = jnp.concatenate([jnp.where(first, v, zero), jnp.where(first, zero, v)], axis=0)
        g_ref[m * PAIR : (m + 1) * PAIR, :] = dot_nt(one_each, v)
    for t in range(OWN, SLOTS):
        g_ref[t * K : (t + 1) * K, :] = top


def to_lanes(g_ref, a_ref):
    count = a_ref.shape[2]
    for i in range(K):
        a_ref[i] = g_ref[pl.ds(i, count, stride=K), :].T


def factor_pairs(a_ref, d_ref, pairs_ref, own_pairs_ref):
    for i in range(K):
        row = a_ref[i]
        d_ref[pl.ds(i, SLOTS, stride=K), :] = jnp.concatenate([row, row], axis=0).T
    first = in_first_half((K, PAIR))
    for t in range(OWN):
        doubled = d_ref[t * K : (t + 1) * K, :]
        high = doubled.astype(BF16).astype(F32)
        low = doubled - high
        pair = jnp.where(first, high, low).astype(BF16)
        pairs_ref[EDGE + t * K : EDGE + (t + 1) * K, :] = pair
        own_pairs_ref[t * PAIR : t * PAIR + K, :] = pair
        own_pairs_ref[t * PAIR + K : (t + 1) * PAIR, :] = jnp.where(first, low, high).astype(BF16)


def place_points(
    first_leaf,
    coords_ref,
    near_ref,
    count_ref,
    source_ref,
    target_ref,
    source_t_ref,
    target_t_ref,
    doubled_ref,
):
    lanes = WIDE * K
    leaf = lax.broadcasted_iota(jnp.int32, (3, lanes), 1) // K
    axis = lax.broadcasted_iota(jnp.int32, (3, lanes), 0)
    corner = jnp.where(
        axis == 0, leaf % 2, jnp.where(axis == 1, leaf // 2 % 2, leaf // LAYER - WIDE // LAYER // 2)
    )
    u = (coords_ref[...] + corner.astype(F32)) * SCALE
    high, middle, low = (part.astype(F32) for part in split3(u))
    norms = [part.astype(F32) for part in split3(-jnp.sum(u * u, axis=0, keepdims=True))]
    ones = jnp.ones((3, lanes), F32)
    own = slice(EDGE, lanes - EDGE)
    for n, (a, b) in enumerate(
        (
            (high, high),
            (high, middle),
            (middle, high),
            (high, low),
            (low, high),
            (middle, middle),
        )
    ):
        target_ref[3 * n : 3 * n + 3, :] = 2.0 * a[:, own]
        source_ref[3 * n : 3 * n + 3, :] = b
    target_ref[18:21, :] = ones[:, own]
    source_ref[21:24, :] = ones
    for n, part in enumerate(norms):
        source_ref[18 + n : 19 + n, :] = part
        target_ref[21 + n : 22 + n, :] = part[:, own]
    source_ref[24:32, :] = jnp.zeros((8, lanes), F32)

    slot = lax.broadcasted_iota(jnp.int32, (NEAR, OWN), 0)
    target = lax.broadcasted_iota(jnp.int32, (NEAR, OWN), 1)
    used = jnp.zeros((NEAR, OWN), jnp.int32)
    for t in range(OWN):
        used = jnp.where(target == t, count_ref[t], used)
    place = near_ref[...] - (first_leaf - LAYER) - target // LAYER * LAYER
    place = jnp.where(slot < used, place, -1)
    window = lax.broadcasted_iota(jnp.int32, (16, OWN), 0)
    bias = jnp.full((16, OWN), OFF, F32)
    for n in range(NEAR):
        bias = jnp.where(place[n : n + 1, :] == window, 0.0, bias)
    spread = lax.broadcasted_iota(jnp.int32, (OWN, OWN * K), 1) // K
    spread = (spread == lax.broadcasted_iota(jnp.int32, (OWN, OWN * K), 0)).astype(F32)
    target_ref[24:40, :] = dot(bias.astype(BF16), spread.astype(BF16))

    target_t_ref[...] = target_ref[...].T.astype(BF16)
    source_t_ref[...] = source_ref[...].T.astype(BF16)
    for t in range(OWN):
        one = target_ref[0:32, t * K : (t + 1) * K]
        doubled_ref[t] = jnp.concatenate([one, one], axis=1).astype(BF16)


def near_layers(layers, source_ref, target_t_ref, vectors_ref, near_out):
    width = LAYER * K
    window = lax.broadcasted_iota(jnp.int32, (16, width), 0)
    column = lax.broadcasted_iota(jnp.int32, (16, width), 1) // K
    for layer in layers:
        total = jnp.zeros((width, vectors_ref.shape[1]), F32)
        for step in range(3):
            at = (layer + 1 + step) * width
            place = (window == column + LAYER * step).astype(F32)
            source = jnp.concatenate([source_ref[0:24, at : at + width], place], axis=0)
            exponent = dot(
                target_t_ref[layer * width : (layer + 1) * width, :], source.astype(BF16)
            )
            weights = kernel_values(exponent).astype(BF16)
            rows = (layer + step) * width
            total = total + dot(weights, vectors_ref[rows : rows + width, :])
        near_out[layer * width : (layer + 1) * width, :] = total.astype(BF16)


def far_leaves(layer, p, at_start, at_end):
    places = []
    for k in range(FAR):
        shift = p - RAD + k + (12 if k + p >= FAR else 0)
        before = max(0, (3 - shift) // 4)
        beyond = max(0, shift // 4)
        place = LAYER * layer + shift
        if before:
            place = place + 15 * at_start * ((7 + before - layer) // 8)
        if beyond:
            place = place - 15 * at_end * ((layer + beyond) // 8)
        places.append(place)
    if isinstance(layer, int):
        places += list(range(11, 15)) if layer == 0 else list(range(17, 21))
    return places


def far_picks(read, names, first_leaf, places):
    values = [read(place + HALO) for place in places]
    picks = []
    for name in names:
        pick = values[0]
        for place, value in zip(places[1:], values[1:]):
            pick = lax.select(name == first_leaf + place, value, pick)
        picks.append(pick)
    return picks


def each_layer(run):
    last = OWN // LAYER - 1
    run(0)

    def step(layer, _):
        run(layer)
        return 0

    lax.fori_loop(1, last, step, 0, unroll=2)
    run(last)


def far_blocks(first_leaf, ends, far_ref, source_t_ref, doubled_ref, block_ref):
    def run(layer):
        for p in range(LAYER):
            t = LAYER * layer + p
            names = [far_ref[f, t] for f in range(FAR)]
            sources = far_picks(
                lambda leaf: leaf_rows(source_t_ref, leaf, K),
                names,
                first_leaf,
                far_leaves(layer, p, *ends),
            )
            exponent = dot(jnp.concatenate(sources, axis=0), doubled_ref[t])
            block_ref[t] = high_low(kernel_values(exponent))

    each_layer(run)


def far_halves(block_ref, own_pairs_ref, half_ref):
    def halves(t, _):
        value = dot_nt(block_ref[t], leaf_rows(own_pairs_ref, t, PAIR))
        half_ref[t] = high_low(add_halves(value) * (1.0 / K))
        return 0

    lax.fori_loop(0, OWN, halves, 0, unroll=4)


def far_products(first_leaf, ends, far_ref, half_ref, pairs_ref, coupling_out):
    def run(layer):
        values = []
        for p in range(LAYER):
            t = LAYER * layer + p
            names = [far_ref[f, t] for f in range(FAR)]
            factors = far_picks(
                lambda leaf: leaf_rows(pairs_ref, leaf, K),
                names,
                first_leaf,
                far_leaves(layer, p, *ends),
            )
            for f in range(FAR):
                half = half_ref[t, f * K : (f + 1) * K, :]
                values.append(add_halves(dot(factors[f], jnp.concatenate([half, half], axis=0))))
        first = in_first_half((K, PAIR))
        both = [jnp.where(first, values[2 * n], values[2 * n + 1]) for n in range(2 * FAR)]
        at = pl.multiple_of(layer * 2 * FAR * PAIR, PAIR)
        coupling_out[:, pl.ds(at, 2 * FAR * PAIR)] = jnp.concatenate(both, axis=1).astype(BF16)

    each_layer(run)


def turned(index, stride, size, by):
    at = lax.rem(index // stride, size)
    return index + (lax.rem(at + by, size) - at) * stride


def upsweep_kernel(
    count_ref,
    far_ref,
    basis_hbm,
    inner_hbm,
    transfer_hbm,
    points_hbm,
    near_hbm,
    vectors_hbm,
    near_hbm_out,
    coupling_hbm_out,
    factor_out,
    group_sum_out,
    root_sum_out,
    near_out,
    coupling_out,
    basis_ref,
    inner_ref,
    transfer_ref,
    near_ref,
    coords_ref,
    vectors_ref,
    g_ref,
    d_ref,
    a_ref,
    x_ref,
    pairs_ref,
    own_pairs_ref,
    source_ref,
    target_ref,
    source_t_ref,
    target_t_ref,
    doubled_ref,
    block_ref,
    half_ref,
    sum_ref,
    got_ref,
    in_sem,
    out_sem,
    send_sem,
    recv_sem,
):
    groups, subs = lax.axis_size("group"), lax.axis_size("sub")
    g, s = lax.axis_index("group"), lax.axis_index("sub")
    me = g * subs + s
    first_leaf = me * OWN
    count = groups * subs
    ends = ((count - me) // count, (me + 1) // count)
    after = lax.rem(me + 1, groups * subs)
    before = lax.rem(me + groups * subs - 1, groups * subs)
    after = (after // subs, lax.rem(after, subs))
    before = (before // subs, lax.rem(before, subs))

    plane = [
        (g, turned(turned(s, 2, 4, x), 8, 4, y)) for x in range(4) for y in range(4) if x or y
    ]
    steps = [(core, z) for core in range(2) for z in (0, 1, 2, 15) if core or z]
    window = [(turned(g, 1, 16, 16 - z), turned(s, 1, 2, core)) for core, z in steps]
    senders = [(turned(g, 1, 16, z), turned(s, 1, 2, core)) for core, z in steps]
    cover = [(turned(g, 1, 16, z), s) for z in (2, 6, 10, 14)]

    barrier = pltpu.get_barrier_semaphore()
    greeted = cover + senders + plane + [after, before]
    for device in greeted:
        pl.semaphore_signal(barrier, inc=1, device_id=device, device_id_type=MESH)

    lanes, rows = points_hbm.shape[1], vectors_hbm.shape[0]
    loads = [
        pltpu.make_async_copy(source, target, in_sem.at[n])
        for n, (source, target) in enumerate(
            (
                (inner_hbm, inner_ref),
                (basis_hbm, basis_ref),
                (transfer_hbm, transfer_ref),
                (points_hbm, coords_ref.at[:, EDGE : EDGE + lanes]),
                (near_hbm, near_ref),
                (vectors_hbm, vectors_ref.at[LAYER * K : LAYER * K + rows]),
            )
        )
    ]
    for load in loads:
        load.start()
    for load in loads[:3]:
        load.wait()

    top = tree_gram(basis_ref, inner_ref, x_ref)
    transfer = transfer_ref[...]
    gram = exact_dot_t(transfer, exact_dot(top, transfer))
    sum_ref[0] = jnp.concatenate([gram[: K // 2], gram[K // 2 :]], axis=1)

    leaf_grams(basis_ref, top, g_ref)
    to_lanes(g_ref, a_ref)
    cholesky_rows(a_ref, range(0, FIRST_PART))

    pl.semaphore_wait(barrier, len(greeted))

    def copy(number, source, target, device):
        return pltpu.make_async_remote_copy(
            src_ref=source,
            dst_ref=target,
            send_sem=send_sem.at[number],
            recv_sem=recv_sem.at[number],
            device_id=device,
            device_id_type=MESH,
        )

    def send(stage, first, devices):
        copies = [
            copy(first + n, sum_ref.at[stage], got_ref.at[first + n], device)
            for n, device in enumerate(devices)
        ]
        for one in copies:
            one.start()
        return copies

    def gather(total, first, copies):
        for n, one in enumerate(copies):
            one.wait()
            total = total + got_ref[first + n]
        return total

    sent = send(0, 0, plane)
    for load in loads[3:]:
        load.wait()
    halos = [
        copy(SUMS, coords_ref.at[:, lanes : lanes + EDGE], coords_ref.at[:, 0:EDGE], after),
        copy(
            SUMS + 1,
            coords_ref.at[:, EDGE : 2 * EDGE],
            coords_ref.at[:, EDGE + lanes : 2 * EDGE + lanes],
            before,
        ),
        copy(
            SUMS + 2,
            vectors_ref.at[rows : rows + LAYER * K],
            vectors_ref.at[0 : LAYER * K],
            after,
        ),
        copy(
            SUMS + 3,
            vectors_ref.at[LAYER * K : 2 * LAYER * K],
            vectors_ref.at[rows + LAYER * K : rows + 2 * LAYER * K],
            before,
        ),
    ]
    for halo in halos:
        halo.start()

    cholesky_rows(a_ref, range(FIRST_PART, 16))
    factor_pairs(a_ref, d_ref, pairs_ref, own_pairs_ref)
    edges = [
        copy(SUMS + 4, pairs_ref.at[OWN * K : OWN * K + EDGE], pairs_ref.at[0:EDGE], after),
        copy(
            SUMS + 5,
            pairs_ref.at[EDGE : 2 * EDGE],
            pairs_ref.at[OWN * K + EDGE : OWN * K + 2 * EDGE],
            before,
        ),
    ]
    for edge in edges:
        edge.start()
    factor_out[...] = exact_dot(d_ref[OWN * K : (OWN + 1) * K, 0:K], transfer)

    sum_ref[1] = gather(sum_ref[0], 0, sent)
    sent = send(1, PLANE, window)
    for halo in halos:
        halo.wait()
    place_points(
        first_leaf,
        coords_ref,
        near_ref,
        count_ref,
        source_ref,
        target_ref,
        source_t_ref,
        target_t_ref,
        doubled_ref,
    )
    far_blocks(first_leaf, ends, far_ref, source_t_ref, doubled_ref, block_ref)
    sum_ref[2] = gather(sum_ref[1], PLANE, sent)
    group_sum_out[...] = sum_ref[1] + got_ref[PLANE + steps.index((1, 0))]
    sent = send(2, PLANE + WINDOW, cover)
    near_layers(range(OWN // LAYER), source_ref, target_t_ref, vectors_ref, near_out)
    near_move = pltpu.make_async_copy(near_out, near_hbm_out, out_sem.at[0])
    near_move.start()
    far_halves(block_ref, own_pairs_ref, half_ref)
    for edge in edges:
        edge.wait()
    far_products(first_leaf, ends, far_ref, half_ref, pairs_ref, coupling_out)
    coupling_move = pltpu.make_async_copy(coupling_out, coupling_hbm_out, out_sem.at[1])
    coupling_move.start()
    root_sum_out[...] = gather(jnp.zeros((K // 2, PAIR), F32), PLANE + WINDOW, sent)
    near_move.wait()
    coupling_move.wait()


def upsweep_call(near_count, far_t, basis_t, inner_t, transfer, points, near_t, vectors):
    whole = pl.BlockSpec(memory_space=pltpu.VMEM)
    scalars = pl.BlockSpec(memory_space=pltpu.SMEM)
    anywhere = pl.BlockSpec(memory_space=pltpu.HBM)
    packed = jax.ShapeDtypeStruct((K // 2, PAIR), F32)
    rows, columns = vectors.shape
    return pl.pallas_call(
        upsweep_kernel,
        out_shape=(
            jax.ShapeDtypeStruct(vectors.shape, BF16),
            jax.ShapeDtypeStruct((K, FAR * OWN * K), BF16),
            jax.ShapeDtypeStruct((K, K), F32),
            packed,
            packed,
        ),
        in_specs=[scalars] * 2 + [anywhere] * INPUTS,
        out_specs=(anywhere,) * 2 + (whole,) * 3,
        scratch_shapes=[
            pltpu.VMEM(vectors.shape, BF16),
            pltpu.VMEM((K, FAR * OWN * K), BF16),
            pltpu.VMEM(basis_t.shape, BF16),
            pltpu.VMEM(inner_t.shape, BF16),
            pltpu.VMEM((K, K), F32),
            pltpu.VMEM(near_t.shape, jnp.int32),
            pltpu.VMEM((3, WIDE * K), F32),
            pltpu.VMEM((rows + 2 * LAYER * K, columns), BF16),
            pltpu.VMEM((SLOTS * K, K), F32),
            pltpu.VMEM((SLOTS * K, PAIR), F32),
            pltpu.VMEM((K, K, SLOTS), F32),
            pltpu.VMEM((3 * K, OWN * K), BF16),
            pltpu.VMEM((WIDE * K, PAIR), BF16),
            pltpu.VMEM((OWN * PAIR, PAIR), BF16),
            pltpu.VMEM((32, WIDE * K), F32),
            pltpu.VMEM((40, OWN * K), F32),
            pltpu.VMEM((WIDE * K, 32), BF16),
            pltpu.VMEM((OWN * K, 40), BF16),
            pltpu.VMEM((OWN, 32, PAIR), BF16),
            pltpu.VMEM((OWN, FAR * K, PAIR), BF16),
            pltpu.VMEM((OWN, FAR * K, PAIR), BF16),
            pltpu.VMEM((3, K // 2, PAIR), F32),
            pltpu.VMEM((SUMS, K // 2, PAIR), F32),
            pltpu.SemaphoreType.DMA((INPUTS,)),
            pltpu.SemaphoreType.DMA((2,)),
            pltpu.SemaphoreType.DMA((COPIES,)),
            pltpu.SemaphoreType.DMA((COPIES,)),
        ],
        compiler_params=pltpu.CompilerParams(
            collective_id=0, has_side_effects=True, vmem_limit_bytes=VMEM_LIMIT
        ),
    )(near_count, far_t, basis_t, inner_t, transfer, points, near_t, vectors)


def unpack(ref):
    return jnp.concatenate([ref[:, :K], ref[:, K:]], axis=0)


def last_kernel(
    group_sum,
    root_sum,
    factor_ref,
    near_ref,
    coupling_ref,
    near_out,
    coupling_out,
    factor_out,
    group_out,
    root_out,
    g_ref,
    a_ref,
    sem,
):
    moves = [
        pltpu.make_async_copy(near_ref, near_out, sem.at[0]),
        pltpu.make_async_copy(coupling_ref, coupling_out, sem.at[1]),
    ]
    for move in moves:
        move.start()
    groups, subs = lax.axis_size("group"), lax.axis_size("sub")
    factor_out[...] = factor_ref[...]
    group = unpack(group_sum[...]) * (1.0 / subs)
    root = unpack(root_sum[...]) * (1.0 / (subs * groups))
    for n in range(8):
        g_ref[n * K : (n + 1) * K, :] = root if n else group
    to_lanes(g_ref, a_ref)
    cholesky_rows(a_ref, range(16))
    for i in range(K):
        g_ref[pl.ds(i, 8, stride=K), :] = a_ref[i].T
    group_out[...] = g_ref[0:K, :]
    root_out[...] = g_ref[K : 2 * K, :]
    for move in moves:
        move.wait()


def last_call(group_sum, root_sum, factor, near, coupling_t):
    whole = pl.BlockSpec(memory_space=pltpu.VMEM)
    anywhere = pl.BlockSpec(memory_space=pl.ANY)
    square = jax.ShapeDtypeStruct((K, K), F32)
    return pl.pallas_call(
        last_kernel,
        out_shape=(
            jax.ShapeDtypeStruct(near.shape, BF16),
            jax.ShapeDtypeStruct(coupling_t.shape, BF16),
            square,
            square,
            square,
        ),
        in_specs=[whole] * 3 + [anywhere] * 2,
        out_specs=(anywhere,) * 2 + (whole,) * 3,
        scratch_shapes=[
            pltpu.VMEM((8 * K, K), F32),
            pltpu.VMEM((K, K, 8), F32),
            pltpu.SemaphoreType.DMA((2,)),
        ],
        compiler_params=pltpu.CompilerParams(vmem_limit_bytes=VMEM_LIMIT),
    )(group_sum, root_sum, factor, near, coupling_t)


def per_device(
    points, leaf_basis, inner_transfer, device_transfer, vectors, near_index, near_count, far_index
):
    near, coupling_t, factor, group_sum, root_sum = upsweep_call(
        near_count,
        far_index.T,
        leaf_basis.T,
        inner_transfer.T,
        device_transfer,
        points,
        near_index.T,
        vectors,
    )
    near_product, coupling_t, device_factor, group_factor, root_factor = last_call(
        group_sum, root_sum, factor, near, coupling_t
    )
    return near_product, coupling_t.T, device_factor, group_factor, root_factor


def solution(mesh):
    rows = P(("group", "sub"), None)
    return jax.shard_map(
        per_device,
        mesh=mesh,
        in_specs=(
            P(None, ("group", "sub")),
            rows,
            rows,
            rows,
            rows,
            rows,
            P(("group", "sub")),
            rows,
        ),
        out_specs=(rows,) * 5,
        check_vma=False,
    )
```

time: 60.2 us -> 118 us (1.96)
  Pallas kernels: 53.7 us -> 117 us
  local copies, waits for them, and re-layouts: 4.84 us -> 0 us
    pallas_call x2, Pallas kernels: 53.7 us -> 117 us  [the longest x1 74 us: last_call(): pl.pallas_call(last_kernel, out_shape=(jax.ShapeDtypeStruct(near.shape, B...]
    unnamed x18 -> x0, local copies, waits for them, and re-layouts: 4.84 us -> none
where the time goes in v3:
time: 118 us
  Pallas kernels  117 us (99%)
    pallas_call x1, Pallas kernels, last_call(): pl.pallas_call(last_kernel, out_shape=(jax.ShapeDtypeStruct(near.shape, B...  74 us
    pallas_call x1, Pallas kernels, upsweep_call(): pl.pallas_call(upsweep_kernel, out_shape=(jax.ShapeDtypeStruct(vectors.sh...  43 us

profile of v3, /device:TPU:1, one launch (start us, length us, event | category | flops | bytes accessed | tf_op | source)
XLA Modules:
  0.0 117.8 jit_solution(4453552039073165054)
XLA Ops:
  0.6 43.0 %shard_map.119 = (bf16[2048,384]{1,0:T(8,128)(2,1)}, bf16[64,6144]{1,0:T(8,128)(2,1)}, f32[64,64]{1,0:T(8,128)}, f32[32,128]{1,0:T(8,128)}, f32[32,128]{1,0:T(8,128)}) custom-call(s32[32]{0:T(128)} %count_ref.1, s32[3,32]{1,0:T(4,128)} %bitcast.8, bf16[64,2048]{1,0:T(8,128)(2,1)} %bitcast.5, bf16[64,1920]{1,0:T(8,128)(2,1)} %bitcast.6, ...), custom_call_target="tpu_custom_call" | custom-call | tf_op jit(solution)/shard_map/pallas_call | solution.py:554
  43.6 74.0 %shard_map.120 = (bf16[2048,384]{1,0:T(8,128)(2,1)}, bf16[64,6144]{1,0:T(8,128)(2,1)}, f32[64,64]{1,0:T(8,128)}, f32[64,64]{1,0:T(8,128)}, f32[64,64]{1,0:T(8,128)}) custom-call(f32[32,128]{1,0:T(8,128)} %get-tuple-element.15.group_sum, f32[32,128]{1,0:T(8,128)} %get-tuple-element.16.root_sum, f32[64,64]{1,0:T(8,128)} %get-tuple-element.17.factor_ref, ...), custom_call_target="tpu_custom_call" | custom-call | tf_op jit(solution)/shard_map/pallas_call | solution.py:645

commit v4 on v3

--- a/solution.py
+++ b/solution.py
@@ -81,7 +81,7 @@
     return x + pltpu.roll(x, K, axis=1)
 
 
-def cholesky_rows(a_ref, blocks):
+def cholesky_rows(a_ref, blocks, unroll=4):
     lanes = a_ref.shape[2]
     for block in blocks:
         first = 4 * block
@@ -95,7 +95,7 @@
             )
 
         if first:
-            rows = lax.fori_loop(0, first, subtract, rows, unroll=4)
+            rows = lax.fori_loop(0, first, subtract, rows, unroll=unroll)
         rows = list(rows)
         index = lax.broadcasted_iota(jnp.int32, (K - start, lanes), 0)
         for q in range(4):
@@ -512,9 +512,7 @@
         edge.start()
     factor_out[...] = exact_dot(d_ref[OWN * K : (OWN + 1) * K, 0:K], transfer)
 
-    sum_ref[1] = gather(sum_ref[0], 0, sent)
-    sent = send(1, PLANE, window)
-    for halo in halos:
+    for halo in halos[:2]:
         halo.wait()
     place_points(
         first_leaf,
@@ -527,11 +525,17 @@
         target_t_ref,
         doubled_ref,
     )
+    near_layers(range(1, 5), source_ref, target_t_ref, vectors_ref, near_out)
+    sum_ref[1] = gather(sum_ref[0], 0, sent)
+    sent = send(1, PLANE, window)
     far_blocks(first_leaf, ends, far_ref, source_t_ref, doubled_ref, block_ref)
+    near_layers(range(5, 7), source_ref, target_t_ref, vectors_ref, near_out)
     sum_ref[2] = gather(sum_ref[1], PLANE, sent)
     group_sum_out[...] = sum_ref[1] + got_ref[PLANE + steps.index((1, 0))]
     sent = send(2, PLANE + WINDOW, cover)
-    near_layers(range(OWN // LAYER), source_ref, target_t_ref, vectors_ref, near_out)
+    for halo in halos[2:]:
+        halo.wait()
+    near_layers((0, 7), source_ref, target_t_ref, vectors_ref, near_out)
     near_move = pltpu.make_async_copy(near_out, near_hbm_out, out_sem.at[0])
     near_move.start()
     far_halves(block_ref, own_pairs_ref, half_ref)
@@ -612,16 +616,22 @@
     factor_out,
     group_out,
     root_out,
+    near_buffer,
+    coupling_buffer,
     g_ref,
     a_ref,
     sem,
 ):
-    moves = [
-        pltpu.make_async_copy(near_ref, near_out, sem.at[0]),
-        pltpu.make_async_copy(coupling_ref, coupling_out, sem.at[1]),
+    arrivals = [
+        pltpu.make_async_copy(near_ref, near_buffer, sem.at[0]),
+        pltpu.make_async_copy(coupling_ref, coupling_buffer, sem.at[1]),
     ]
-    for move in moves:
-        move.start()
+    departures = [
+        pltpu.make_async_copy(near_buffer, near_out, sem.at[2]),
+        pltpu.make_async_copy(coupling_buffer, coupling_out, sem.at[3]),
+    ]
+    for arrival in arrivals:
+        arrival.start()
     groups, subs = lax.axis_size("group"), lax.axis_size("sub")
     factor_out[...] = factor_ref[...]
     group = unpack(group_sum[...]) * (1.0 / subs)
@@ -629,13 +639,17 @@
     for n in range(8):
         g_ref[n * K : (n + 1) * K, :] = root if n else group
     to_lanes(g_ref, a_ref)
-    cholesky_rows(a_ref, range(16))
+    cholesky_rows(a_ref, range(8), unroll=True)
+    for arrival, departure in zip(arrivals, departures):
+        arrival.wait()
+        departure.start()
+    cholesky_rows(a_ref, range(8, 16), unroll=True)
     for i in range(K):
         g_ref[pl.ds(i, 8, stride=K), :] = a_ref[i].T
     group_out[...] = g_ref[0:K, :]
     root_out[...] = g_ref[K : 2 * K, :]
-    for move in moves:
-        move.wait()
+    for departure in departures:
+        departure.wait()
 
 
 def last_call(group_sum, root_sum, factor, near, coupling_t):
@@ -654,9 +668,11 @@
         in_specs=[whole] * 3 + [anywhere] * 2,
         out_specs=(anywhere,) * 2 + (whole,) * 3,
         scratch_shapes=[
+            pltpu.VMEM(near.shape, BF16),
+            pltpu.VMEM(coupling_t.shape, BF16),
             pltpu.VMEM((8 * K, K), F32),
             pltpu.VMEM((K, K, 8), F32),
-            pltpu.SemaphoreType.DMA((2,)),
+            pltpu.SemaphoreType.DMA((4,)),
         ],
         compiler_params=pltpu.CompilerParams(vmem_limit_bytes=VMEM_LIMIT),
     )(group_sum, root_sum, factor, near, coupling_t)

time: 118 us -> 45.8 us (0.39)
  Pallas kernels: 117 us -> 44.4 us
    pallas_call x1, Pallas kernels: 74 us -> 4.65 us  [last_call(): pl.pallas_call(last_kernel, out_shape=(jax.ShapeDtypeStruct(near.shape, B...]
    pallas_call x1, Pallas kernels: 43 us -> 39.8 us  [upsweep_call(): pl.pallas_call(upsweep_kernel, out_shape=(jax.ShapeDtypeStruct(vectors.sh...]
where the time goes in v4:
time: 45.8 us; the launch traced here: 45.2 us
  Pallas kernels  44.4 us (97%)
  between operations  0.8 us (2%)
    pallas_call x1, Pallas kernels, upsweep_call(): pl.pallas_call(upsweep_kernel, out_shape=(jax.ShapeDtypeStruct(vectors.sh...  39.8 us
    pallas_call x1, Pallas kernels, last_call(): pl.pallas_call(last_kernel, out_shape=(jax.ShapeDtypeStruct(near.shape, B...  4.65 us

profile of v4, /device:TPU:1, one launch (start us, length us, event | category | flops | bytes accessed | tf_op | source)
XLA Modules:
  0.0 45.2 jit_solution(7960962596706334650)
XLA Ops:
  0.6 39.8 %shard_map.119 = (bf16[2048,384]{1,0:T(8,128)(2,1)}, bf16[64,6144]{1,0:T(8,128)(2,1)}, f32[64,64]{1,0:T(8,128)}, f32[32,128]{1,0:T(8,128)}, f32[32,128]{1,0:T(8,128)}) custom-call(s32[32]{0:T(128)} %count_ref.1, s32[3,32]{1,0:T(4,128)} %bitcast.8, bf16[64,2048]{1,0:T(8,128)(2,1)} %bitcast.5, bf16[64,1920]{1,0:T(8,128)(2,1)} %bitcast.6, ...), custom_call_target="tpu_custom_call" | custom-call | tf_op jit(solution)/shard_map/pallas_call | solution.py:558
  40.4 4.6 %shard_map.120 = (bf16[2048,384]{1,0:T(8,128)(2,1)}, bf16[64,6144]{1,0:T(8,128)(2,1)}, f32[64,64]{1,0:T(8,128)}, f32[64,64]{1,0:T(8,128)}, f32[64,64]{1,0:T(8,128)}) custom-call(f32[32,128]{1,0:T(8,128)} %get-tuple-element.15.group_sum, f32[32,128]{1,0:T(8,128)} %get-tuple-element.16.root_sum, f32[64,64]{1,0:T(8,128)} %get-tuple-element.17.factor_ref, ...), custom_call_target="tpu_custom_call" | custom-call | tf_op jit(solution)/shard_map/pallas_call | solution.py:659

commit v5 on v4

--- a/solution.py
+++ b/solution.py
@@ -402,13 +402,13 @@
     after = (after // subs, lax.rem(after, subs))
     before = (before // subs, lax.rem(before, subs))
 
-    plane = [
-        (g, turned(turned(s, 2, 4, x), 8, 4, y)) for x in range(4) for y in range(4) if x or y
-    ]
-    steps = [(core, z) for core in range(2) for z in (0, 1, 2, 15) if core or z]
+    hops = [(x, y) for x in (2, 1, 3, 0) for y in (2, 1, 3, 0) if x or y]
+    hops = sorted(hops, key=lambda hop: -sum(min(h, 4 - h) for h in hop))
+    plane = [(g, turned(turned(s, 2, 4, x), 8, 4, y)) for x, y in hops]
+    steps = [(core, z) for z in (2, 1, 15, 0) for core in (1, 0) if core or z]
     window = [(turned(g, 1, 16, 16 - z), turned(s, 1, 2, core)) for core, z in steps]
     senders = [(turned(g, 1, 16, z), turned(s, 1, 2, core)) for core, z in steps]
-    cover = [(turned(g, 1, 16, z), s) for z in (2, 6, 10, 14)]
+    cover = [(turned(g, 1, 16, z), s) for z in (6, 10, 2, 14)]
 
     barrier = pltpu.get_barrier_semaphore()
     greeted = cover + senders + plane + [after, before]

time: 45.8 us -> 45.2 us (0.987)
  no operation moved by 1% of the time
where the time goes in v5:
time: 45.2 us; the launch traced here: 44.9 us
  Pallas kernels  44.1 us (98%)
  between operations  0.8 us (2%)
    pallas_call x1, Pallas kernels, upsweep_call(): pl.pallas_call(upsweep_kernel, out_shape=(jax.ShapeDtypeStruct(vectors.sh...  39.5 us
    pallas_call x1, Pallas kernels, last_call(): pl.pallas_call(last_kernel, out_shape=(jax.ShapeDtypeStruct(near.shape, B...  4.65 us

profile of v5, /device:TPU:1, one launch (start us, length us, event | category | flops | bytes accessed | tf_op | source)
XLA Modules:
  0.0 44.9 jit_solution(2756738174653591568)
XLA Ops:
  0.6 39.5 %shard_map.119 = (bf16[2048,384]{1,0:T(8,128)(2,1)}, bf16[64,6144]{1,0:T(8,128)(2,1)}, f32[64,64]{1,0:T(8,128)}, f32[32,128]{1,0:T(8,128)}, f32[32,128]{1,0:T(8,128)}) custom-call(s32[32]{0:T(128)} %count_ref.1, s32[3,32]{1,0:T(4,128)} %bitcast.8, bf16[64,2048]{1,0:T(8,128)(2,1)} %bitcast.5, bf16[64,1920]{1,0:T(8,128)(2,1)} %bitcast.6, ...), custom_call_target="tpu_custom_call" | custom-call | tf_op jit(solution)/shard_map/pallas_call | solution.py:558
  40.1 4.6 %shard_map.120 = (bf16[2048,384]{1,0:T(8,128)(2,1)}, bf16[64,6144]{1,0:T(8,128)(2,1)}, f32[64,64]{1,0:T(8,128)}, f32[64,64]{1,0:T(8,128)}, f32[64,64]{1,0:T(8,128)}) custom-call(f32[32,128]{1,0:T(8,128)} %get-tuple-element.15.group_sum, f32[32,128]{1,0:T(8,128)} %get-tuple-element.16.root_sum, f32[64,64]{1,0:T(8,128)} %get-tuple-element.17.factor_ref, ...), custom_call_target="tpu_custom_call" | custom-call | tf_op jit(solution)/shard_map/pallas_call | solution.py:659
